TPU v7x, 512 devices: a whole 4x4x16 slice. The times are simulated.
512 devices in a mesh: width: 8 (over x, core), vocab: 64 (over y, z).
Axes of the slice: x: 4, y: 4, z: 16, core: 2. Of those that a mesh axis runs over, the one named last changes fastest.
Arguments:
- hidden: bfloat16 [1024, 16384], P('vocab', 'width'), may hold values from -6 to 6
- weight: bfloat16 [16384, 65536], P('width', 'vocab'), may hold values from -1 to 1
- policy: bfloat16 [1024, 65536], P('width', 'vocab'), may hold values from -480 to 480
Outputs:
- divergence: float32 [1024], P('width')
- gradient: float32 [1024, 65536], P('width', 'vocab')
All inputs are finite; a program needn't handle non-finite values.
Results may differ from a plain program's by a relative error of at most 0.00035.
Values may be sent and summed in bfloat16 or wider, within the bound.
No kernel may reach another device: no remote copies, remote signals or barrier semaphores. Data moves between devices by JAX's collectives and lax.ppermute only.
A program may use at most 64 MiB of HBM per device.

v0:
```python
import jax
import jax.numpy as jnp
from jax import lax
from jax.sharding import Mesh, PartitionSpec as P

Z = ("zh", "zl")


def spread(value, axes, groups=None):
    size = len(groups[0]) if groups else lax.axis_size(axes)
    return lax.all_to_all(
        jnp.broadcast_to(value[None], (size, *value.shape)), axes, 0, 0, axis_index_groups=groups
    )


def along_z(value, by):
    return lax.ppermute(value, Z, [((i + by) % 16, i) for i in range(16)])


def from_core(value):
    return lax.ppermute(value, "core", [(0, 1), (1, 0)])


def send_x(value, by):
    return lax.ppermute(value, "x", [(i, (i + by) % 4) for i in range(4)])


def product(rows, weight):
    return jnp.dot(rows, weight, preferred_element_type=jnp.float32)


def local_lse(values):
    top = jnp.max(values, axis=1)
    powers = jnp.exp(values - top[:, None])
    return top + jnp.log(jnp.sum(powers, axis=1)), powers


def joint_lse(parts):
    top = jnp.max(parts, axis=0)
    return top + jnp.log(jnp.sum(jnp.exp(parts - top), axis=0))


def body(hidden, weight, policy):
    own_first = [[0, 1, 2, 3], [6, 7, 4, 5]]
    coarse = spread(hidden, ("core", "zh"), own_first)
    first, second = coarse[:, :8], coarse[:, 8:]

    by_owner = [[4 * x + (x + k) % 4 for k in range(4)] for x in range(4)]
    c_own = spread(second, ("x", "y"), by_owner)
    c_own = c_own.reshape(4, 2, 16, 2048).transpose(1, 0, 2, 3).reshape(128, 2048)
    near = [first] + [along_z(first, k) for k in (2, 1, -1)]
    a_own = jnp.stack([near[n] for n in (0, 2, 1, 3)], axis=1).reshape(2, 64, 2048)

    c_plus = along_z(c_own, 1)
    c_minus = along_z(c_own, -1)
    a_all = spread(a_own, ("x", "y"), by_owner)
    c_two_a = along_z(c_own[:64], 2)
    c_two_b = along_z(c_own[64:], -2)

    def chips(parts):
        total = parts[0]
        for k in (2, 1, 3):
            total += send_x(parts[k], k)
        return total


    def early(half):
        return jnp.concatenate([part[half] for part in (c_own, c_plus, c_minus)])

    away = from_core(product(early(slice(64, 128)), weight))
    early = product(early(slice(0, 64)), weight) + away
    early = early.reshape(3, 4, 16, 1024).transpose(1, 0, 2, 3).reshape(4, 48, 1024)
    early = chips(early)

    c_away = from_core(product(c_two_b, weight))
    a_send = product(a_all[:, 1].reshape(256, 2048), weight)
    a_away = from_core(a_send)
    c_late = (product(c_two_a, weight) + c_away).reshape(4, 16, 1024)
    a_late = (product(a_all[:, 0].reshape(256, 2048), weight) + a_away).reshape(4, 64, 1024)
    late = chips(jnp.concatenate([c_late, a_late], axis=1))

    c_logits = [early[:16], early[16:32], late[:16], early[32:]]
    c_logits = jnp.stack([part.reshape(2, 8, 1024) for part in c_logits], axis=1)
    a_logits = late[16:].reshape(2, 4, 8, 1024)
    logits = jnp.stack([a_logits, c_logits], axis=2)
    logits = jnp.roll(logits, lax.axis_index("zl"), axis=1).reshape(128, 1024)

    values = policy.astype(jnp.float32)
    policy_lse, powers = local_lse(values)
    difference = values - logits
    mean = jnp.sum(powers * difference, axis=1) / jnp.sum(powers, axis=1)
    parts = jnp.stack([local_lse(logits)[0], policy_lse, mean])
    parts = spread(parts, ("y", "zh", "zl"))
    reference_lse = joint_lse(parts[:, 0])
    policy_lse = joint_lse(parts[:, 1])
    mean = jnp.sum(jnp.exp(parts[:, 1] - policy_lse) * parts[:, 2], axis=0)
    divergence = mean - policy_lse + reference_lse
    gradient = jnp.exp(values - policy_lse[:, None]) * (difference - mean[:, None])
    return (divergence, gradient)


def solution(mesh):
    split = Mesh(mesh.devices.reshape(4, 2, 4, 4, 4), ("x", "core", "y", "zh", "zl"))
    rows, columns = ("y", "zh", "zl"), ("x", "core")

    def step(*args):
        return body(*args)

    step = jax.shard_map(
        step,
        mesh=split,
        in_specs=(P(rows, columns), P(columns, rows), P(columns, rows)),
        out_specs=(P(columns), P(columns, rows)),
        check_vma=False,
    )
    return step
```

profile of v0, /device:TPU:8, one launch (start us, length us, event | category | flops | bytes accessed | tf_op | source)
XLA Modules:
  0.0 163.0 jit_solution(12450265225787506738)
XLA Ops:
  0.6 0.9 broadcast_in_dim.10
  1.5 31.0 %all_to_all.20 = bf16[4,16,2048]{2,1,0:T(8,128)(2,1)S(1)} all-to-all(bf16[4,16,2048]{2,1,0:T(8,128)(2,1)S(1)} %broadcast_in_dim.10), channel_id=1, replica_groups={{0,4,8,12},{72,76,64,68},{1,5,9,13},{73,77,65,69},{2,6,10,14},{74,78,66..., dimensions={0} | all-to-all | bytes 524288 | tf_op jit(solution)/shard_map/all_to_all | solution.py:11
  32.5 0.8 broadcast_in_dim.11
  33.3 4.9 %all-to-all-start.1 = ((bf16[4,4,8,2048]{3,2,1,0:T(8,128)(2,1)}), bf16[4,4,8,2048]{3,2,1,0:T(8,128)(2,1)S(1)}, u32[]{:S(2)}, u32[]{:S(2)}) async-start(bf16[4,4,8,2048]{3,2,1,0:T(8,128)(2,1)} %broadcast_in_dim.11), calls=%async_computation.1 | async-start | bytes 1048576 | tf_op jit(solution)/shard_map/all_to_all | solution.py:11
  38.3 3.5 %collective-permute-start.4 = (bf16[4,8,2048]{2,1,0:T(8,128)(2,1)S(1)}, bf16[4,8,2048]{2,1,0:T(8,128)(2,1)S(1)}, u32[]{:S(2)}, u32[]{:S(2)}) collective-permute-start(bf16[4,8,2048]{2,1,0:T(8,128)(2,1)S(1)} %get-tuple-element.22), channel_id=1, source_target_pairs={{2,0},{3,1},{4,2},{5,3},{6,4},{7,5},{8,6},{9,7},{10,8},{11,9},{12,... | collective-permute-start | bytes 393224 | tf_op jit(solution)/shard_map/ppermute | solution.py:17
  41.7 2.9 %collective-permute-start.5 = (bf16[4,8,2048]{2,1,0:T(8,128)(2,1)S(1)}, bf16[4,8,2048]{2,1,0:T(8,128)(2,1)S(1)}, u32[]{:S(2)}, u32[]{:S(2)}) collective-permute-start(bf16[4,8,2048]{2,1,0:T(8,128)(2,1)S(1)} %get-tuple-element.22), channel_id=1, source_target_pairs={{15,0},{0,1},{1,2},{2,3},{3,4},{4,5},{5,6},{6,7},{7,8},{8,9},{9,10... | collective-permute-start | bytes 393224 | tf_op jit(solution)/shard_map/ppermute | solution.py:17
  44.6 4.2 %collective-permute-start.3 = (bf16[4,8,2048]{2,1,0:T(8,128)(2,1)S(1)}, bf16[4,8,2048]{2,1,0:T(8,128)(2,1)S(1)}, u32[]{:S(2)}, u32[]{:S(2)}) collective-permute-start(bf16[4,8,2048]{2,1,0:T(8,128)(2,1)S(1)} %get-tuple-element.22), channel_id=1, source_target_pairs={{1,0},{2,1},{3,2},{4,3},{5,4},{6,5},{7,6},{8,7},{9,8},{10,9},{11,1... | collective-permute-start | bytes 393224 | tf_op jit(solution)/shard_map/ppermute | solution.py:17
  48.8 0.0 all-to-all-done.1
  48.8 0.8 fusion.38
  49.7 2.6 %collective-permute-start.1 = (bf16[64,2048]{1,0:T(8,128)(2,1)}, bf16[64,2048]{1,0:T(8,128)(2,1)}, u32[]{:S(2)}, u32[]{:S(2)}) collective-permute-start(bf16[64,2048]{1,0:T(8,128)(2,1)} %bitcast.4), channel_id=1, source_target_pairs={{14,0},{15,1},{0,2},{1,3},{2,4},{3,5},{4,6},{5,7},{6,8},{7,9},{8,1... | collective-permute-start | bytes 786440 | tf_op jit(solution)/shard_map/ppermute | solution.py:17
  52.3 3.7 %collective-permute-start.10 = (bf16[128,2048]{1,0:T(8,128)(2,1)S(1)}, bf16[128,2048]{1,0:T(8,128)(2,1)S(1)}, u32[]{:S(2)}, u32[]{:S(2)}) collective-permute-start(bf16[128,2048]{1,0:T(8,128)(2,1)S(1)} %bitcast.103), channel_id=1, source_target_pairs={{1,0},{2,1},{3,2},{4,3},{5,4},{6,5},{7,6},{8,7},{9,8},{10,9},{11,1... | collective-permute-start | bytes 1572872 | tf_op jit(solution)/shard_map/ppermute | solution.py:17
  56.0 0.0 collective-permute-done.4
  56.0 0.0 collective-permute-done.5
  56.0 0.0 collective-permute-done.3
  56.0 0.1 pad_maximum_fusion
  56.1 1.6 broadcast_in_dim.13
  57.7 4.8 %all-to-all-start.2 = ((bf16[4,2,64,2048]{3,2,1,0:T(8,128)(2,1)}), bf16[4,2,64,2048]{3,2,1,0:T(8,128)(2,1)S(1)}, u32[]{:S(2)}, u32[]{:S(2)}) async-start(bf16[4,2,64,2048]{3,2,1,0:T(8,128)(2,1)} %broadcast_in_dim.13), calls=%async_computation.2 | async-start | bytes 4194304 | tf_op jit(solution)/shard_map/all_to_all | solution.py:11
  62.5 2.6 %collective-permute-start.11 = (bf16[128,2048]{1,0:T(8,128)(2,1)S(1)}, bf16[128,2048]{1,0:T(8,128)(2,1)S(1)}, u32[]{:S(2)}, u32[]{:S(2)}) collective-permute-start(bf16[128,2048]{1,0:T(8,128)(2,1)S(1)} %bitcast.104), channel_id=1, source_target_pairs={{15,0},{0,1},{1,2},{2,3},{3,4},{4,5},{5,6},{6,7},{7,8},{8,9},{9,10... | collective-permute-start | bytes 1572872 | tf_op jit(solution)/shard_map/ppermute | solution.py:17
  65.1 5.2 %collective-permute-start = (bf16[64,2048]{1,0:T(8,128)(2,1)}, bf16[64,2048]{1,0:T(8,128)(2,1)S(1)}, u32[]{:S(2)}, u32[]{:S(2)}) collective-permute-start(bf16[64,2048]{1,0:T(8,128)(2,1)} %bitcast.110), channel_id=1, source_target_pairs={{2,0},{3,1},{4,2},{5,3},{6,4},{7,5},{8,6},{9,7},{10,8},{11,9},{12,... | collective-permute-start | bytes 786440 | tf_op jit(solution)/shard_map/ppermute | solution.py:17
  70.3 3.8 %fusion.42 = f32[64,1024]{1,0:T(8,128)} fusion(bf16[64,2048]{1,0:T(8,128)(2,1)} %collective-permute-done.1, bf16[2048,1024]{1,0:T(8,128)(2,1)} %param.4), kind=kOutput, calls=%fused_computation.76 | convolution fusion | flops 268435456 | bytes 4718592 | tf_op jit(solution)/shard_map/dot_general | solution.py:29
  74.1 1.9 %collective-permute-start.2 = (f32[64,1024]{1,0:T(8,128)}, f32[64,1024]{1,0:T(8,128)}, u32[]{:S(2)}, u32[]{:S(2)}) collective-permute-start(f32[64,1024]{1,0:T(8,128)} %fusion.42), channel_id=1, source_target_pairs={{0,64},{64,0},{1,65},{65,1},{2,66},{66,2},{3,67},{67,3},{4,68},{68... | collective-permute-start | bytes 786440 | tf_op jit(solution)/shard_map/ppermute | solution.py:21
  76.0 0.0 collective-permute-done.10
  76.0 0.7 fusion.39
  76.8 0.7 fusion.40
  77.5 2.9 %fusion.5 = f32[192,1024]{1,0:T(8,128)} fusion(bf16[2048,1024]{1,0:T(8,128)(2,1)S(1)} %copy-done, bf16[64,2048]{1,0:T(8,128)(2,1)S(1)} %get-tuple-element.20, bf16[64,2048]{1,0:T(8,128)(2,1)S(1)} %get-tuple-element.18, bf16[64,2048]{1,0:T(8,128)(2,1)} %bitcast.4), kind=kOutput, calls=%fused_computation.18 | convolution fusion | flops 807665664 | bytes 5767168 | tf_op jit(solution)/shard_map/dot_general | solution.py:29
  80.4 2.4 %collective-permute-start.12 = (f32[192,1024]{1,0:T(8,128)}, f32[192,1024]{1,0:T(8,128)}, u32[]{:S(2)}, u32[]{:S(2)}) collective-permute-start(f32[192,1024]{1,0:T(8,128)} %fusion.5), channel_id=1, source_target_pairs={{0,64},{64,0},{1,65},{65,1},{2,66},{66,2},{3,67},{67,3},{4,68},{68... | collective-permute-start | bytes 2359304 | tf_op jit(solution)/shard_map/ppermute | solution.py:21
  82.8 1.3 all-to-all-done.2
  84.1 0.2 fusion.36
  84.3 0.0 copy-start.3
  84.3 2.0 %copy-done.1 = bf16[2048,1024]{1,0:T(8,128)(2,1)S(1)} copy-done((bf16[2048,1024]{1,0:T(8,128)(2,1)S(1)}, bf16[2048,1024]{1,0:T(8,128)(2,1)}, u32[]{:S(2)}) %copy-start.1) | copy-done | bytes 4194328
  86.3 2.3 %fusion.43 = f32[256,1024]{1,0:T(8,128)} fusion(bf16[256,2048]{1,0:T(8,128)(2,1)S(1)} %bitcast.101, bf16[2048,1024]{1,0:T(8,128)(2,1)S(1)} %copy-done.1), kind=kOutput, calls=%fused_computation.77 | convolution fusion | flops 1073741824 | bytes 6291456 | tf_op jit(solution)/shard_map/dot_general | solution.py:29
  88.5 2.0 %collective-permute-start.6 = (f32[256,1024]{1,0:T(8,128)}, f32[256,1024]{1,0:T(8,128)}, u32[]{:S(2)}, u32[]{:S(2)}) collective-permute-start(f32[256,1024]{1,0:T(8,128)} %fusion.43), channel_id=1, source_target_pairs={{0,64},{64,0},{1,65},{65,1},{2,66},{66,2},{3,67},{67,3},{4,68},{68... | collective-permute-start | bytes 3145736 | tf_op jit(solution)/shard_map/ppermute | solution.py:21
  90.6 0.1 reduce_max.42
  90.8 0.0 copy-start.2
  90.8 0.0 collective-permute-done
  90.8 0.0 collective-permute-done.2
  90.8 3.2 %convolution_add_fusion.2 = f32[64,1024]{1,0:T(8,128)S(1)} fusion(f32[64,1024]{1,0:T(8,128)} %collective-permute-done.2, bf16[64,2048]{1,0:T(8,128)(2,1)S(1)} %collective-permute-done, bf16[2048,1024]{1,0:T(8,128)(2,1)} %param.4), kind=kOutput, calls=%fused_computation.8 | convolution fusion | flops 268500992 | bytes 4980736 | tf_op jit(solution)/shard_map/dot_general | solution.py:29
  94.0 0.2 copy-done.2
  94.3 2.2 %convolution_add_fusion.1 = f32[192,1024]{1,0:T(8,128)S(1)} fusion(f32[192,1024]{1,0:T(8,128)} %collective-permute-done.12, bf16[2048,1024]{1,0:T(8,128)(2,1)S(1)} %copy-done.2, bf16[64,2048]{1,0:T(8,128)(2,1)S(1)} %copy-done.6, bf16[64,2048]{1,0:T(8,128)(2,1)S(1)} %copy-done.5, bf16[64,2048]{1,0:T(8,128)(2,1)S(1)} %bitcast.111), kind=kOutput, calls=%fused_computation.7 | convolution fusion | flops 807862272 | bytes 6553600 | tf_op jit(solution)/shard_map/dot_general | solution.py:29
  96.5 0.1 fusion.37
  96.5 4.7 %collective-permute-start.13 = (f32[48,1024]{1,0:T(8,128)S(1)}, f32[48,1024]{1,0:T(8,128)S(1)}, u32[]{:S(2)}, u32[]{:S(2)}) collective-permute-start(f32[48,1024]{1,0:T(8,128)S(1)} %bitcast.114), channel_id=1, source_target_pairs={{0,256},{128,384},{256,0},{384,128},{1,257},{129,385},{257,1},{385... | collective-permute-start | bytes 589832 | tf_op jit(solution)/shard_map/ppermute | solution.py:25
  101.2 2.3 %collective-permute-start.14 = (f32[48,1024]{1,0:T(8,128)S(1)}, f32[48,1024]{1,0:T(8,128)S(1)}, u32[]{:S(2)}, u32[]{:S(2)}) collective-permute-start(f32[48,1024]{1,0:T(8,128)S(1)} %bitcast.113), channel_id=1, source_target_pairs={{0,128},{128,256},{256,384},{384,0},{1,129},{129,257},{257,385},{3... | collective-permute-start | bytes 589832 | tf_op jit(solution)/shard_map/ppermute | solution.py:25
  103.6 4.7 %collective-permute-start.15 = (f32[48,1024]{1,0:T(8,128)S(1)}, f32[48,1024]{1,0:T(8,128)S(1)}, u32[]{:S(2)}, u32[]{:S(2)}) collective-permute-start(f32[48,1024]{1,0:T(8,128)S(1)} %bitcast.112), channel_id=1, source_target_pairs={{0,384},{128,0},{256,128},{384,256},{1,385},{129,1},{257,129},{385... | collective-permute-start | bytes 589832 | tf_op jit(solution)/shard_map/ppermute | solution.py:25
  108.3 0.0 collective-permute-done.6
  108.3 2.5 %convolution_add_fusion = f32[256,1024]{1,0:T(8,128)S(1)} fusion(f32[256,1024]{1,0:T(8,128)} %collective-permute-done.6, bf16[256,2048]{1,0:T(8,128)(2,1)S(1)} %bitcast.100, bf16[2048,1024]{1,0:T(8,128)(2,1)S(1)} %copy-done.2), kind=kOutput, calls=%fused_computation.6 | convolution fusion | flops 1074003968 | bytes 7340032 | tf_op jit(solution)/shard_map/dot_general | solution.py:29
  110.9 0.1 fusion.28
  110.9 1.9 %collective-permute-start.7 = (f32[80,1024]{1,0:T(8,128)S(1)}, f32[80,1024]{1,0:T(8,128)S(1)}, u32[]{:S(2)}, u32[]{:S(2)}) collective-permute-start(f32[80,1024]{1,0:T(8,128)S(1)} %get-tuple-element.8), channel_id=1, source_target_pairs={{0,256},{128,384},{256,0},{384,128},{1,257},{129,385},{257,1},{385... | collective-permute-start | bytes 983048 | tf_op jit(solution)/shard_map/ppermute | solution.py:25
  112.9 3.2 %collective-permute-start.8 = (f32[80,1024]{1,0:T(8,128)S(1)}, f32[80,1024]{1,0:T(8,128)S(1)}, u32[]{:S(2)}, u32[]{:S(2)}) collective-permute-start(f32[80,1024]{1,0:T(8,128)S(1)} %get-tuple-element.10), channel_id=1, source_target_pairs={{0,128},{128,256},{256,384},{384,0},{1,129},{129,257},{257,385},{3... | collective-permute-start | bytes 983048 | tf_op jit(solution)/shard_map/ppermute | solution.py:25
  116.0 0.0 collective-permute-done.13
  116.1 3.9 %collective-permute-start.9 = (f32[80,1024]{1,0:T(8,128)S(1)}, f32[80,1024]{1,0:T(8,128)S(1)}, u32[]{:S(2)}, u32[]{:S(2)}) collective-permute-start(f32[80,1024]{1,0:T(8,128)S(1)} %get-tuple-element.9), channel_id=1, source_target_pairs={{0,384},{128,0},{256,128},{384,256},{1,385},{129,1},{257,129},{385... | collective-permute-start | bytes 983048 | tf_op jit(solution)/shard_map/ppermute | solution.py:25
  119.9 0.0 collective-permute-done.14
  120.0 0.0 collective-permute-done.15
  120.0 4.9 %collective-permute-done.7 = f32[80,1024]{1,0:T(8,128)S(1)} collective-permute-done((f32[80,1024]{1,0:T(8,128)S(1)}, f32[80,1024]{1,0:T(8,128)S(1)}, u32[]{:S(2)}, u32[]{:S(2)}) %collective-permute-start.7) | collective-permute-done | bytes 327712 | tf_op jit(solution)/shard_map/ppermute | solution.py:25
  125.0 5.7 %collective-permute-done.8 = f32[80,1024]{1,0:T(8,128)S(1)} collective-permute-done((f32[80,1024]{1,0:T(8,128)S(1)}, f32[80,1024]{1,0:T(8,128)S(1)}, u32[]{:S(2)}, u32[]{:S(2)}) %collective-permute-start.8) | collective-permute-done | bytes 327712 | tf_op jit(solution)/shard_map/ppermute | solution.py:25
  130.6 0.0 collective-permute-done.9
  130.7 0.1 fusion.26
  130.8 0.2 fusion.34
  131.0 0.2 exponential_reduce_fusion
  131.2 0.1 add.92
  131.3 0.3 fusion.13
  131.7 29.6 %all_to_all.21 = f32[64,3,128]{2,1,0:T(4,128)S(1)} all-to-all(f32[64,3,128]{2,1,0:T(4,128)S(1)} %broadcast_in_dim.14), channel_id=1, replica_groups=mesh['x'=4,'core'=2,'y'=4,'zh'=4,'zl'=4] {'y','zh','zl'}, dimensions={0} | all-to-all | bytes 196608 | tf_op jit(solution)/shard_map/all_to_all | solution.py:11
  161.3 0.1 fusion.41
  161.5 1.0 fusion.16
  162.5 0.5 add_add_fusion
  (30 shorter events, 0.4 us)
Async XLA Ops:
  33.3 15.5 %all-to-all-start.1 = ((bf16[4,4,8,2048]{3,2,1,0:T(8,128)(2,1)}), bf16[4,4,8,2048]{3,2,1,0:T(8,128)(2,1)S(1)}, u32[]{:S(2)}, u32[]{:S(2)}) async-start(bf16[4,4,8,2048]{3,2,1,0:T(8,128)(2,1)} %broadcast_in_dim.11), calls=%async_computation.1 | async-start | bytes 1048576 | tf_op jit(solution)/shard_map/all_to_all | solution.py:11
  38.3 17.7 %collective-permute-start.4 = (bf16[4,8,2048]{2,1,0:T(8,128)(2,1)S(1)}, bf16[4,8,2048]{2,1,0:T(8,128)(2,1)S(1)}, u32[]{:S(2)}, u32[]{:S(2)}) collective-permute-start(bf16[4,8,2048]{2,1,0:T(8,128)(2,1)S(1)} %get-tuple-element.22), channel_id=1, source_target_pairs={{2,0},{3,1},{4,2},{5,3},{6,4},{7,5},{8,6},{9,7},{10,8},{11,9},{12,... | collective-permute-start | bytes 393224 | tf_op jit(solution)/shard_map/ppermute | solution.py:17
  41.7 14.2 %collective-permute-start.5 = (bf16[4,8,2048]{2,1,0:T(8,128)(2,1)S(1)}, bf16[4,8,2048]{2,1,0:T(8,128)(2,1)S(1)}, u32[]{:S(2)}, u32[]{:S(2)}) collective-permute-start(bf16[4,8,2048]{2,1,0:T(8,128)(2,1)S(1)} %get-tuple-element.22), channel_id=1, source_target_pairs={{15,0},{0,1},{1,2},{2,3},{3,4},{4,5},{5,6},{6,7},{7,8},{8,9},{9,10... | collective-permute-start | bytes 393224 | tf_op jit(solution)/shard_map/ppermute | solution.py:17
  44.6 11.4 %collective-permute-start.3 = (bf16[4,8,2048]{2,1,0:T(8,128)(2,1)S(1)}, bf16[4,8,2048]{2,1,0:T(8,128)(2,1)S(1)}, u32[]{:S(2)}, u32[]{:S(2)}) collective-permute-start(bf16[4,8,2048]{2,1,0:T(8,128)(2,1)S(1)} %get-tuple-element.22), channel_id=1, source_target_pairs={{1,0},{2,1},{3,2},{4,3},{5,4},{6,5},{7,6},{8,7},{9,8},{10,9},{11,1... | collective-permute-start | bytes 393224 | tf_op jit(solution)/shard_map/ppermute | solution.py:17
  49.7 20.6 %collective-permute-start.1 = (bf16[64,2048]{1,0:T(8,128)(2,1)}, bf16[64,2048]{1,0:T(8,128)(2,1)}, u32[]{:S(2)}, u32[]{:S(2)}) collective-permute-start(bf16[64,2048]{1,0:T(8,128)(2,1)} %bitcast.4), channel_id=1, source_target_pairs={{14,0},{15,1},{0,2},{1,3},{2,4},{3,5},{4,6},{5,7},{6,8},{7,9},{8,1... | collective-permute-start | bytes 786440 | tf_op jit(solution)/shard_map/ppermute | solution.py:17
  52.3 23.8 %collective-permute-start.10 = (bf16[128,2048]{1,0:T(8,128)(2,1)S(1)}, bf16[128,2048]{1,0:T(8,128)(2,1)S(1)}, u32[]{:S(2)}, u32[]{:S(2)}) collective-permute-start(bf16[128,2048]{1,0:T(8,128)(2,1)S(1)} %bitcast.103), channel_id=1, source_target_pairs={{1,0},{2,1},{3,2},{4,3},{5,4},{6,5},{7,6},{8,7},{9,8},{10,9},{11,1... | collective-permute-start | bytes 1572872 | tf_op jit(solution)/shard_map/ppermute | solution.py:17
  57.7 26.4 %all-to-all-start.2 = ((bf16[4,2,64,2048]{3,2,1,0:T(8,128)(2,1)}), bf16[4,2,64,2048]{3,2,1,0:T(8,128)(2,1)S(1)}, u32[]{:S(2)}, u32[]{:S(2)}) async-start(bf16[4,2,64,2048]{3,2,1,0:T(8,128)(2,1)} %broadcast_in_dim.13), calls=%async_computation.2 | async-start | bytes 4194304 | tf_op jit(solution)/shard_map/all_to_all | solution.py:11
  62.5 15.1 %copy-start = (bf16[2048,1024]{1,0:T(8,128)(2,1)S(1)}, bf16[2048,1024]{1,0:T(8,128)(2,1)}, u32[]{:S(2)}) copy-start(bf16[2048,1024]{1,0:T(8,128)(2,1)} %param.4) | copy-start | bytes 12582916
  62.5 14.3 %collective-permute-start.11 = (bf16[128,2048]{1,0:T(8,128)(2,1)S(1)}, bf16[128,2048]{1,0:T(8,128)(2,1)S(1)}, u32[]{:S(2)}, u32[]{:S(2)}) collective-permute-start(bf16[128,2048]{1,0:T(8,128)(2,1)S(1)} %bitcast.104), channel_id=1, source_target_pairs={{15,0},{0,1},{1,2},{2,3},{3,4},{4,5},{5,6},{6,7},{7,8},{8,9},{9,10... | collective-permute-start | bytes 1572872 | tf_op jit(solution)/shard_map/ppermute | solution.py:17
  65.1 25.7 %collective-permute-start = (bf16[64,2048]{1,0:T(8,128)(2,1)}, bf16[64,2048]{1,0:T(8,128)(2,1)S(1)}, u32[]{:S(2)}, u32[]{:S(2)}) collective-permute-start(bf16[64,2048]{1,0:T(8,128)(2,1)} %bitcast.110), channel_id=1, source_target_pairs={{2,0},{3,1},{4,2},{5,3},{6,4},{7,5},{8,6},{9,7},{10,8},{11,9},{12,... | collective-permute-start | bytes 786440 | tf_op jit(solution)/shard_map/ppermute | solution.py:17
  74.1 16.7 %collective-permute-start.2 = (f32[64,1024]{1,0:T(8,128)}, f32[64,1024]{1,0:T(8,128)}, u32[]{:S(2)}, u32[]{:S(2)}) collective-permute-start(f32[64,1024]{1,0:T(8,128)} %fusion.42), channel_id=1, source_target_pairs={{0,64},{64,0},{1,65},{65,1},{2,66},{66,2},{3,67},{67,3},{4,68},{68... | collective-permute-start | bytes 786440 | tf_op jit(solution)/shard_map/ppermute | solution.py:21
  80.4 13.6 %collective-permute-start.12 = (f32[192,1024]{1,0:T(8,128)}, f32[192,1024]{1,0:T(8,128)}, u32[]{:S(2)}, u32[]{:S(2)}) collective-permute-start(f32[192,1024]{1,0:T(8,128)} %fusion.5), channel_id=1, source_target_pairs={{0,64},{64,0},{1,65},{65,1},{2,66},{66,2},{3,67},{67,3},{4,68},{68... | collective-permute-start | bytes 2359304 | tf_op jit(solution)/shard_map/ppermute | solution.py:21
  84.1 2.2 %copy-start.1 = (bf16[2048,1024]{1,0:T(8,128)(2,1)S(1)}, bf16[2048,1024]{1,0:T(8,128)(2,1)}, u32[]{:S(2)}) copy-start(bf16[2048,1024]{1,0:T(8,128)(2,1)} %param.4) | copy-start | bytes 12582916
  84.3 6.3 %copy-start.3 = (bf16[128,1024]{1,0:T(8,128)(2,1)S(1)}, bf16[128,1024]{1,0:T(8,128)(2,1)}, u32[]{:S(2)}) copy-start(bf16[128,1024]{1,0:T(8,128)(2,1)} %param.5) | copy-start | bytes 786436
  88.5 5.5 %copy-start.4 = (bf16[1,4,16,2048]{3,2,0,1:T(8,128)(2,1)S(1)}, bf16[1,4,16,2048]{3,2,0,1:T(8,128)(2,1)}, u32[]{:S(2)}) copy-start(bf16[1,4,16,2048]{3,2,0,1:T(8,128)(2,1)} %get-tuple-element.15) | copy-start | bytes 786436
  88.5 5.5 %copy-start.5 = (bf16[64,2048]{1,0:T(8,128)(2,1)S(1)}, bf16[64,2048]{1,0:T(8,128)(2,1)}, u32[]{:S(2)}) copy-start(bf16[64,2048]{1,0:T(8,128)(2,1)} %get-tuple-element.17) | copy-start | bytes 786436
  88.5 5.5 %copy-start.6 = (bf16[64,2048]{1,0:T(8,128)(2,1)S(1)}, bf16[64,2048]{1,0:T(8,128)(2,1)}, u32[]{:S(2)}) copy-start(bf16[64,2048]{1,0:T(8,128)(2,1)} %get-tuple-element.19) | copy-start | bytes 786436
  88.5 19.8 %collective-permute-start.6 = (f32[256,1024]{1,0:T(8,128)}, f32[256,1024]{1,0:T(8,128)}, u32[]{:S(2)}, u32[]{:S(2)}) collective-permute-start(f32[256,1024]{1,0:T(8,128)} %fusion.43), channel_id=1, source_target_pairs={{0,64},{64,0},{1,65},{65,1},{2,66},{66,2},{3,67},{67,3},{4,68},{68... | collective-permute-start | bytes 3145736 | tf_op jit(solution)/shard_map/ppermute | solution.py:21
  90.8 3.5 %copy-start.2 = (bf16[2048,1024]{1,0:T(8,128)(2,1)S(1)}, bf16[2048,1024]{1,0:T(8,128)(2,1)}, u32[]{:S(2)}) copy-start(bf16[2048,1024]{1,0:T(8,128)(2,1)} %param.4) | copy-start | bytes 12582916
  96.5 19.5 %collective-permute-start.13 = (f32[48,1024]{1,0:T(8,128)S(1)}, f32[48,1024]{1,0:T(8,128)S(1)}, u32[]{:S(2)}, u32[]{:S(2)}) collective-permute-start(f32[48,1024]{1,0:T(8,128)S(1)} %bitcast.114), channel_id=1, source_target_pairs={{0,256},{128,384},{256,0},{384,128},{1,257},{129,385},{257,1},{385... | collective-permute-start | bytes 589832 | tf_op jit(solution)/shard_map/ppermute | solution.py:25
  101.2 18.7 %collective-permute-start.14 = (f32[48,1024]{1,0:T(8,128)S(1)}, f32[48,1024]{1,0:T(8,128)S(1)}, u32[]{:S(2)}, u32[]{:S(2)}) collective-permute-start(f32[48,1024]{1,0:T(8,128)S(1)} %bitcast.113), channel_id=1, source_target_pairs={{0,128},{128,256},{256,384},{384,0},{1,129},{129,257},{257,385},{3... | collective-permute-start | bytes 589832 | tf_op jit(solution)/shard_map/ppermute | solution.py:25
  103.6 16.4 %collective-permute-start.15 = (f32[48,1024]{1,0:T(8,128)S(1)}, f32[48,1024]{1,0:T(8,128)S(1)}, u32[]{:S(2)}, u32[]{:S(2)}) collective-permute-start(f32[48,1024]{1,0:T(8,128)S(1)} %bitcast.112), channel_id=1, source_target_pairs={{0,384},{128,0},{256,128},{384,256},{1,385},{129,1},{257,129},{385... | collective-permute-start | bytes 589832 | tf_op jit(solution)/shard_map/ppermute | solution.py:25
  110.9 14.0 %collective-permute-start.7 = (f32[80,1024]{1,0:T(8,128)S(1)}, f32[80,1024]{1,0:T(8,128)S(1)}, u32[]{:S(2)}, u32[]{:S(2)}) collective-permute-start(f32[80,1024]{1,0:T(8,128)S(1)} %get-tuple-element.8), channel_id=1, source_target_pairs={{0,256},{128,384},{256,0},{384,128},{1,257},{129,385},{257,1},{385... | collective-permute-start | bytes 983048 | tf_op jit(solution)/shard_map/ppermute | solution.py:25
  112.9 17.8 %collective-permute-start.8 = (f32[80,1024]{1,0:T(8,128)S(1)}, f32[80,1024]{1,0:T(8,128)S(1)}, u32[]{:S(2)}, u32[]{:S(2)}) collective-permute-start(f32[80,1024]{1,0:T(8,128)S(1)} %get-tuple-element.10), channel_id=1, source_target_pairs={{0,128},{128,256},{256,384},{384,0},{1,129},{129,257},{257,385},{3... | collective-permute-start | bytes 983048 | tf_op jit(solution)/shard_map/ppermute | solution.py:25
  116.1 14.6 %collective-permute-start.9 = (f32[80,1024]{1,0:T(8,128)S(1)}, f32[80,1024]{1,0:T(8,128)S(1)}, u32[]{:S(2)}, u32[]{:S(2)}) collective-permute-start(f32[80,1024]{1,0:T(8,128)S(1)} %get-tuple-element.9), channel_id=1, source_target_pairs={{0,384},{128,0},{256,128},{384,256},{1,385},{129,1},{257,129},{385... | collective-permute-start | bytes 983048 | tf_op jit(solution)/shard_map/ppermute | solution.py:25
where the time goes:
time: 164 us; the launch traced here: 163 us
  starting transfers between devices  61.3 us (37%)
  blocking collectives  60.6 us (37%)
  matrix products  16.8 us (10%)
  waiting for transfers between devices  12 us (7%)
  local copies, waits for them, and re-layouts  8.41 us (5%)
  other arithmetic  2.82 us (2%)
    all_to_all x2, blocking collectives, spread(): lax.all_to_all(jnp.broadcast_to(value[None], (size, *value.shape)), axes,...  60.6 us
    ppermute x7, starting transfers between devices, along_z(): return lax.ppermute(value, Z, [((i + by) % 16, i) for i in range(16)])  24.6 us
    ppermute x6, starting transfers between devices, send_x(): return lax.ppermute(value, 'x', [(i, (i + by) % 4) for i in range(4)])  20.7 us
    dot_general x6, matrix products, product(): return jnp.dot(rows, weight, preferred_element_type=jnp.float32)  16.8 us
    ppermute x6, waiting for transfers between devices, send_x(): return lax.ppermute(value, 'x', [(i, (i + by) % 4) for i in range(4)])  10.6 us
    all_to_all x2, starting transfers between devices, spread(): lax.all_to_all(jnp.broadcast_to(value[None], (size, *value.shape)), axes,...  9.71 us
    ppermute x3, starting transfers between devices, from_core(): return lax.ppermute(value, 'core', [(0, 1), (1, 0)])  6.34 us
    broadcast_in_dim x4, local copies, waits for them, and re-layouts, spread(): jnp.broadcast_to(value[None], (size, *value.shape))  3.32 us
  transfers between devices with their start and end apart: 18, of which 3 were waited for; matrix products, arithmetic and copies ran while one was open for 13% of the time, Pallas kernels for 0%

commit v1 on v0

--- a/solution.py
+++ b/solution.py
@@ -63,25 +63,24 @@
             total += send_x(parts[k], k)
         return total
 
+    def early(half):
+        return product(jnp.concatenate([part[half] for part in (c_own, c_plus, c_minus)]), weight)
 
-    def early(half):
-        return jnp.concatenate([part[half] for part in (c_own, c_plus, c_minus)])
+    away = from_core(early(slice(64, 128)))
+    early = (early(slice(0, 64)) + away).reshape(3, 4, 16, 1024)
 
-    away = from_core(product(early(slice(64, 128)), weight))
-    early = product(early(slice(0, 64)), weight) + away
-    early = early.reshape(3, 4, 16, 1024).transpose(1, 0, 2, 3).reshape(4, 48, 1024)
-    early = chips(early)
+    def late(c_rows, a_rows):
+        rows = jnp.concatenate([c_rows.reshape(4, 16, 2048), a_rows], axis=1)
+        return product(rows.reshape(320, 2048), weight)
 
-    c_away = from_core(product(c_two_b, weight))
-    a_send = product(a_all[:, 1].reshape(256, 2048), weight)
-    a_away = from_core(a_send)
-    c_late = (product(c_two_a, weight) + c_away).reshape(4, 16, 1024)
-    a_late = (product(a_all[:, 0].reshape(256, 2048), weight) + a_away).reshape(4, 64, 1024)
-    late = chips(jnp.concatenate([c_late, a_late], axis=1))
+    away = from_core(late(c_two_b, a_all[:, 1]))
+    late = (late(c_two_a, a_all[:, 0]) + away).reshape(4, 80, 1024)
+    sums = [jnp.concatenate([*early[:, k], late[k]]) for k in range(4)]
+    sums = chips(sums)
 
-    c_logits = [early[:16], early[16:32], late[:16], early[32:]]
+    c_logits = [sums[:16], sums[16:32], sums[48:64], sums[32:48]]
     c_logits = jnp.stack([part.reshape(2, 8, 1024) for part in c_logits], axis=1)
-    a_logits = late[16:].reshape(2, 4, 8, 1024)
+    a_logits = sums[64:].reshape(2, 4, 8, 1024)
     logits = jnp.stack([a_logits, c_logits], axis=2)
     logits = jnp.roll(logits, lax.axis_index("zl"), axis=1).reshape(128, 1024)
 

time: 164 us -> 169 us (1.030)
  the two profiles are of different devices: /device:TPU:8 before, /device:TPU:4 now
where the time goes in v1:
time: 169 us; the launch traced here: 168 us
  blocking collectives  58.1 us (34%)
  starting transfers between devices  49.5 us (29%)
  waiting for transfers between devices  38.3 us (23%)
  matrix products  9.48 us (6%)
  local copies, waits for them, and re-layouts  7.77 us (5%)
  other arithmetic  3.85 us (2%)
    all_to_all x2, blocking collectives, spread(): lax.all_to_all(jnp.broadcast_to(value[None], (size, *value.shape)), axes,...  58.1 us
    ppermute x7, starting transfers between devices, along_z(): return lax.ppermute(value, Z, [((i + by) % 16, i) for i in range(16)])  25.4 us
    ppermute x3, waiting for transfers between devices, send_x(): return lax.ppermute(value, 'x', [(i, (i + by) % 4) for i in range(4)])  19.2 us
    ppermute x7, waiting for transfers between devices, along_z(): return lax.ppermute(value, Z, [((i + by) % 16, i) for i in range(16)])  19.1 us
    all_to_all x2, starting transfers between devices, spread(): lax.all_to_all(jnp.broadcast_to(value[None], (size, *value.shape)), axes,...  11.4 us
    dot_general x4, matrix products, product(): return jnp.dot(rows, weight, preferred_element_type=jnp.float32)  9.48 us
    ppermute x3, starting transfers between devices, send_x(): return lax.ppermute(value, 'x', [(i, (i + by) % 4) for i in range(4)])  8.34 us
    ppermute x2, starting transfers between devices, from_core(): return lax.ppermute(value, 'core', [(0, 1), (1, 0)])  4.32 us
  transfers between devices with their start and end apart: 14, of which 6 were waited for; matrix products, arithmetic and copies ran while one was open for 8% of the time, Pallas kernels for 0%

profile of v1, /device:TPU:4, one launch (start us, length us, event | category | flops | bytes accessed | tf_op | source)
XLA Modules:
  0.0 168.0 jit_solution(5980985105051060474)
XLA Ops:
  0.6 0.9 broadcast_in_dim.10
  1.5 31.0 %all_to_all.20 = bf16[4,16,2048]{2,1,0:T(8,128)(2,1)S(1)} all-to-all(bf16[4,16,2048]{2,1,0:T(8,128)(2,1)S(1)} %broadcast_in_dim.10), channel_id=1, replica_groups={{0,4,8,12},{72,76,64,68},{1,5,9,13},{73,77,65,69},{2,6,10,14},{74,78,66..., dimensions={0} | all-to-all | bytes 524288 | tf_op jit(solution)/shard_map/all_to_all | solution.py:11
  32.5 0.8 broadcast_in_dim.11
  33.3 6.6 %all-to-all-start.1 = ((bf16[4,4,8,2048]{3,2,1,0:T(8,128)(2,1)}), bf16[4,4,8,2048]{3,2,1,0:T(8,128)(2,1)S(1)}, u32[]{:S(2)}, u32[]{:S(2)}) async-start(bf16[4,4,8,2048]{3,2,1,0:T(8,128)(2,1)} %broadcast_in_dim.11), calls=%async_computation.1 | async-start | bytes 1048576 | tf_op jit(solution)/shard_map/all_to_all | solution.py:11
  40.0 1.9 %collective-permute-start.4 = (bf16[4,8,2048]{2,1,0:T(8,128)(2,1)S(1)}, bf16[4,8,2048]{2,1,0:T(8,128)(2,1)S(1)}, u32[]{:S(2)}, u32[]{:S(2)}) collective-permute-start(bf16[4,8,2048]{2,1,0:T(8,128)(2,1)S(1)} %get-tuple-element.36), channel_id=1, source_target_pairs={{1,0},{2,1},{3,2},{4,3},{5,4},{6,5},{7,6},{8,7},{9,8},{10,9},{11,1... | collective-permute-start | bytes 393224 | tf_op jit(solution)/shard_map/ppermute | solution.py:17
  41.9 3.5 %collective-permute-start.5 = (bf16[4,8,2048]{2,1,0:T(8,128)(2,1)S(1)}, bf16[4,8,2048]{2,1,0:T(8,128)(2,1)S(1)}, u32[]{:S(2)}, u32[]{:S(2)}) collective-permute-start(bf16[4,8,2048]{2,1,0:T(8,128)(2,1)S(1)} %get-tuple-element.36), channel_id=1, source_target_pairs={{2,0},{3,1},{4,2},{5,3},{6,4},{7,5},{8,6},{9,7},{10,8},{11,9},{12,... | collective-permute-start | bytes 393224 | tf_op jit(solution)/shard_map/ppermute | solution.py:17
  45.4 3.9 %collective-permute-start.6 = (bf16[4,8,2048]{2,1,0:T(8,128)(2,1)S(1)}, bf16[4,8,2048]{2,1,0:T(8,128)(2,1)S(1)}, u32[]{:S(2)}, u32[]{:S(2)}) collective-permute-start(bf16[4,8,2048]{2,1,0:T(8,128)(2,1)S(1)} %get-tuple-element.36), channel_id=1, source_target_pairs={{15,0},{0,1},{1,2},{2,3},{3,4},{4,5},{5,6},{6,7},{7,8},{8,9},{9,10... | collective-permute-start | bytes 393224 | tf_op jit(solution)/shard_map/ppermute | solution.py:17
  49.3 0.0 all-to-all-done.1
  49.4 3.1 %collective-permute-start = (bf16[128,2048]{1,0:T(8,128)(2,1)S(1)}, bf16[128,2048]{1,0:T(8,128)(2,1)}, u32[]{:S(2)}, u32[]{:S(2)}) collective-permute-start(bf16[128,2048]{1,0:T(8,128)(2,1)S(1)} %bitcast.94), channel_id=1, source_target_pairs={{1,0},{2,1},{3,2},{4,3},{5,4},{6,5},{7,6},{8,7},{9,8},{10,9},{11,1... | collective-permute-start | bytes 1572872 | tf_op jit(solution)/shard_map/ppermute | solution.py:17
  52.5 0.0 collective-permute-done.4
  52.5 0.8 collective-permute-done.5
  53.4 0.1 collective-permute-done.6
  53.5 0.1 pad_maximum_fusion.2
  53.5 1.6 broadcast_in_dim.13
  55.1 4.8 %all-to-all-start.2 = ((bf16[4,2,64,2048]{3,2,1,0:T(8,128)(2,1)}), bf16[4,2,64,2048]{3,2,1,0:T(8,128)(2,1)S(1)}, u32[]{:S(2)}, u32[]{:S(2)}) async-start(bf16[4,2,64,2048]{3,2,1,0:T(8,128)(2,1)} %broadcast_in_dim.13), calls=%async_computation.2 | async-start | bytes 4194304 | tf_op jit(solution)/shard_map/all_to_all | solution.py:11
  59.9 2.7 %collective-permute-start.1 = (bf16[128,2048]{1,0:T(8,128)(2,1)S(1)}, bf16[128,2048]{1,0:T(8,128)(2,1)S(1)}, u32[]{:S(2)}, u32[]{:S(2)}) collective-permute-start(bf16[128,2048]{1,0:T(8,128)(2,1)S(1)} %bitcast.95), channel_id=1, source_target_pairs={{15,0},{0,1},{1,2},{2,3},{3,4},{4,5},{5,6},{6,7},{7,8},{8,9},{9,10... | collective-permute-start | bytes 1572872 | tf_op jit(solution)/shard_map/ppermute | solution.py:17
  62.6 0.7 fusion.29
  63.4 6.3 %collective-permute-start.7 = (bf16[64,2048]{1,0:T(8,128)(2,1)}, bf16[64,2048]{1,0:T(8,128)(2,1)S(1)}, u32[]{:S(2)}, u32[]{:S(2)}) collective-permute-start(bf16[64,2048]{1,0:T(8,128)(2,1)} %bitcast.5), channel_id=1, source_target_pairs={{14,0},{15,1},{0,2},{1,3},{2,4},{3,5},{4,6},{5,7},{6,8},{7,9},{8,1... | collective-permute-start | bytes 786440 | tf_op jit(solution)/shard_map/ppermute | solution.py:17
  69.7 0.0 collective-permute-done
  69.7 1.1 fusion.27
  70.8 9.9 %collective-permute-done.1 = bf16[128,2048]{1,0:T(8,128)(2,1)S(1)} collective-permute-done((bf16[128,2048]{1,0:T(8,128)(2,1)S(1)}, bf16[128,2048]{1,0:T(8,128)(2,1)S(1)}, u32[]{:S(2)}, u32[]{:S(2)}) %collective-permute-start.1) | collective-permute-done | bytes 524320 | tf_op jit(solution)/shard_map/ppermute | solution.py:17
  80.7 4.2 %fusion.5 = f32[192,1024]{1,0:T(8,128)} fusion(bf16[2048,1024]{1,0:T(8,128)(2,1)} %param.4, bf16[64,2048]{1,0:T(8,128)(2,1)S(1)} %get-tuple-element.31, bf16[64,2048]{1,0:T(8,128)(2,1)S(1)} %get-tuple-element.29, bf16[64,2048]{1,0:T(8,128)(2,1)} %bitcast.5), kind=kOutput, calls=%fused_computation.15 | convolution fusion | flops 807665664 | bytes 5767168 | tf_op jit(solution)/shard_map/dot_general | solution.py:29
  84.9 1.9 %collective-permute-start.2 = (f32[192,1024]{1,0:T(8,128)}, f32[192,1024]{1,0:T(8,128)}, u32[]{:S(2)}, u32[]{:S(2)}) collective-permute-start(f32[192,1024]{1,0:T(8,128)} %fusion.5), channel_id=1, source_target_pairs={{0,64},{64,0},{1,65},{65,1},{2,66},{66,2},{3,67},{67,3},{4,68},{68... | collective-permute-start | bytes 2359304 | tf_op jit(solution)/shard_map/ppermute | solution.py:21
  86.8 0.0 all-to-all-done.2
  86.9 0.0 copy-start.1
  86.9 0.1 slice_bitcast_fusion.1
  87.0 0.0 collective-permute-done.7
  87.0 0.1 pad_maximum_fusion.1
  87.1 1.9 %copy-done.1 = bf16[2048,1024]{1,0:T(8,128)(2,1)S(1)} copy-done((bf16[2048,1024]{1,0:T(8,128)(2,1)S(1)}, bf16[2048,1024]{1,0:T(8,128)(2,1)}, u32[]{:S(2)}) %copy-start.1) | copy-done | bytes 4194328
  89.1 1.6 fusion.32
  90.6 2.4 %collective-permute-start.8 = (f32[320,1024]{1,0:T(8,128)S(1)}, f32[320,1024]{1,0:T(8,128)S(1)}, u32[]{:S(2)}, u32[]{:S(2)}) collective-permute-start(f32[320,1024]{1,0:T(8,128)S(1)} %fusion.32), channel_id=1, source_target_pairs={{0,64},{64,0},{1,65},{65,1},{2,66},{66,2},{3,67},{67,3},{4,68},{68... | collective-permute-start | bytes 3932168 | tf_op jit(solution)/shard_map/ppermute | solution.py:21
  93.0 3.9 %collective-permute-start.3 = (bf16[64,2048]{1,0:T(8,128)(2,1)S(1)}, bf16[64,2048]{1,0:T(8,128)(2,1)S(1)}, u32[]{:S(2)}, u32[]{:S(2)}) collective-permute-start(bf16[64,2048]{1,0:T(8,128)(2,1)S(1)} %bitcast.103), channel_id=1, source_target_pairs={{2,0},{3,1},{4,2},{5,3},{6,4},{7,5},{8,6},{9,7},{10,8},{11,9},{12,... | collective-permute-start | bytes 786440 | tf_op jit(solution)/shard_map/ppermute | solution.py:17
  97.0 0.0 collective-permute-done.2
  97.0 2.2 %convolution_add_fusion.1 = f32[192,1024]{1,0:T(8,128)S(1)} fusion(f32[192,1024]{1,0:T(8,128)} %collective-permute-done.2, bf16[2048,1024]{1,0:T(8,128)(2,1)S(1)} %copy-done.1, bf16[64,2048]{1,0:T(8,128)(2,1)S(1)} %get-tuple-element.30, bf16[64,2048]{1,0:T(8,128)(2,1)S(1)} %get-tuple-element.28, bf16[64,2048]{1,0:T(8,128)(2,1)S(1)} %bitcast.104), kind=kOutput, calls=%fused_computation.3 | convolution fusion | flops 807862272 | bytes 6553600 | tf_op jit(solution)/shard_map/dot_general | solution.py:29
  99.2 0.1 slice_bitcast_fusion.17
  99.2 8.2 %collective-permute-done.3 = bf16[64,2048]{1,0:T(8,128)(2,1)S(1)} collective-permute-done((bf16[64,2048]{1,0:T(8,128)(2,1)S(1)}, bf16[64,2048]{1,0:T(8,128)(2,1)S(1)}, u32[]{:S(2)}, u32[]{:S(2)}) %collective-permute-start.3) | collective-permute-done | bytes 262176 | tf_op jit(solution)/shard_map/ppermute | solution.py:17
  107.5 0.1 pad_maximum_fusion
  107.5 0.0 collective-permute-done.8
  107.6 1.6 convolution_add_fusion
  109.1 0.1 fusion.26
  109.3 0.0 copy-start
  109.3 2.1 %collective-permute-start.9 = (f32[128,1024]{1,0:T(8,128)S(1)}, f32[128,1024]{1,0:T(8,128)S(1)}, u32[]{:S(2)}, u32[]{:S(2)}) collective-permute-start(f32[128,1024]{1,0:T(8,128)S(1)} %pad_maximum_fusion.3), channel_id=1, source_target_pairs={{0,256},{128,384},{256,0},{384,128},{1,257},{129,385},{257,1},{385... | collective-permute-start | bytes 1572872 | tf_op jit(solution)/shard_map/ppermute | solution.py:25
  111.4 2.9 %collective-permute-start.10 = (f32[128,1024]{1,0:T(8,128)S(1)}, f32[128,1024]{1,0:T(8,128)S(1)}, u32[]{:S(2)}, u32[]{:S(2)}) collective-permute-start(f32[128,1024]{1,0:T(8,128)S(1)} %pad_maximum_fusion.4), channel_id=1, source_target_pairs={{0,128},{128,256},{256,384},{384,0},{1,129},{129,257},{257,385},{3... | collective-permute-start | bytes 1572872 | tf_op jit(solution)/shard_map/ppermute | solution.py:25
  114.4 0.8 pad_maximum_fusion.5
  115.2 3.4 %collective-permute-start.11 = (f32[128,1024]{1,0:T(8,128)}, f32[128,1024]{1,0:T(8,128)S(1)}, u32[]{:S(2)}, u32[]{:S(2)}) collective-permute-start(f32[128,1024]{1,0:T(8,128)} %pad_maximum_fusion.5), channel_id=1, source_target_pairs={{0,384},{128,0},{256,128},{384,256},{1,385},{129,1},{257,129},{385... | collective-permute-start | bytes 1572872 | tf_op jit(solution)/shard_map/ppermute | solution.py:25
  118.6 0.0 copy-done
  118.6 0.1 reduce_max.42
  118.7 9.0 %collective-permute-done.9 = f32[128,1024]{1,0:T(8,128)S(1)} collective-permute-done((f32[128,1024]{1,0:T(8,128)S(1)}, f32[128,1024]{1,0:T(8,128)S(1)}, u32[]{:S(2)}, u32[]{:S(2)}) %collective-permute-start.9) | collective-permute-done | bytes 524320 | tf_op jit(solution)/shard_map/ppermute | solution.py:25
  127.7 10.2 %collective-permute-done.10 = f32[128,1024]{1,0:T(8,128)S(1)} collective-permute-done((f32[128,1024]{1,0:T(8,128)S(1)}, f32[128,1024]{1,0:T(8,128)S(1)}, u32[]{:S(2)}, u32[]{:S(2)}) %collective-permute-start.10) | collective-permute-done | bytes 524320 | tf_op jit(solution)/shard_map/ppermute | solution.py:25
  137.9 0.0 collective-permute-done.11
  137.9 0.2 fusion.21
  138.2 0.2 fusion.24
  138.4 0.2 exponential_reduce_fusion
  138.7 0.1 add.76
  138.8 0.3 fusion.13
  139.1 27.1 %all_to_all.21 = f32[64,3,128]{2,1,0:T(4,128)S(1)} all-to-all(f32[64,3,128]{2,1,0:T(4,128)S(1)} %broadcast_in_dim.14), channel_id=1, replica_groups=mesh['x'=4,'core'=2,'y'=4,'zh'=4,'zl'=4] {'y','zh','zl'}, dimensions={0} | all-to-all | bytes 196608 | tf_op jit(solution)/shard_map/all_to_all | solution.py:11
  166.2 0.1 fusion.31
  166.5 1.0 fusion.16
  167.5 0.5 add_add_fusion
  (20 shorter events, 0.5 us)
Async XLA Ops:
  33.3 16.0 %all-to-all-start.1 = ((bf16[4,4,8,2048]{3,2,1,0:T(8,128)(2,1)}), bf16[4,4,8,2048]{3,2,1,0:T(8,128)(2,1)S(1)}, u32[]{:S(2)}, u32[]{:S(2)}) async-start(bf16[4,4,8,2048]{3,2,1,0:T(8,128)(2,1)} %broadcast_in_dim.11), calls=%async_computation.1 | async-start | bytes 1048576 | tf_op jit(solution)/shard_map/all_to_all | solution.py:11
  40.0 12.5 %collective-permute-start.4 = (bf16[4,8,2048]{2,1,0:T(8,128)(2,1)S(1)}, bf16[4,8,2048]{2,1,0:T(8,128)(2,1)S(1)}, u32[]{:S(2)}, u32[]{:S(2)}) collective-permute-start(bf16[4,8,2048]{2,1,0:T(8,128)(2,1)S(1)} %get-tuple-element.36), channel_id=1, source_target_pairs={{1,0},{2,1},{3,2},{4,3},{5,4},{6,5},{7,6},{8,7},{9,8},{10,9},{11,1... | collective-permute-start | bytes 393224 | tf_op jit(solution)/shard_map/ppermute | solution.py:17
  41.9 11.5 %collective-permute-start.5 = (bf16[4,8,2048]{2,1,0:T(8,128)(2,1)S(1)}, bf16[4,8,2048]{2,1,0:T(8,128)(2,1)S(1)}, u32[]{:S(2)}, u32[]{:S(2)}) collective-permute-start(bf16[4,8,2048]{2,1,0:T(8,128)(2,1)S(1)} %get-tuple-element.36), channel_id=1, source_target_pairs={{2,0},{3,1},{4,2},{5,3},{6,4},{7,5},{8,6},{9,7},{10,8},{11,9},{12,... | collective-permute-start | bytes 393224 | tf_op jit(solution)/shard_map/ppermute | solution.py:17
  45.4 8.1 %collective-permute-start.6 = (bf16[4,8,2048]{2,1,0:T(8,128)(2,1)S(1)}, bf16[4,8,2048]{2,1,0:T(8,128)(2,1)S(1)}, u32[]{:S(2)}, u32[]{:S(2)}) collective-permute-start(bf16[4,8,2048]{2,1,0:T(8,128)(2,1)S(1)} %get-tuple-element.36), channel_id=1, source_target_pairs={{15,0},{0,1},{1,2},{2,3},{3,4},{4,5},{5,6},{6,7},{7,8},{8,9},{9,10... | collective-permute-start | bytes 393224 | tf_op jit(solution)/shard_map/ppermute | solution.py:17
  49.4 20.3 %collective-permute-start = (bf16[128,2048]{1,0:T(8,128)(2,1)S(1)}, bf16[128,2048]{1,0:T(8,128)(2,1)}, u32[]{:S(2)}, u32[]{:S(2)}) collective-permute-start(bf16[128,2048]{1,0:T(8,128)(2,1)S(1)} %bitcast.94), channel_id=1, source_target_pairs={{1,0},{2,1},{3,2},{4,3},{5,4},{6,5},{7,6},{8,7},{9,8},{10,9},{11,1... | collective-permute-start | bytes 1572872 | tf_op jit(solution)/shard_map/ppermute | solution.py:17
  55.1 31.7 %all-to-all-start.2 = ((bf16[4,2,64,2048]{3,2,1,0:T(8,128)(2,1)}), bf16[4,2,64,2048]{3,2,1,0:T(8,128)(2,1)S(1)}, u32[]{:S(2)}, u32[]{:S(2)}) async-start(bf16[4,2,64,2048]{3,2,1,0:T(8,128)(2,1)} %broadcast_in_dim.13), calls=%async_computation.2 | async-start | bytes 4194304 | tf_op jit(solution)/shard_map/all_to_all | solution.py:11
  59.9 20.8 %collective-permute-start.1 = (bf16[128,2048]{1,0:T(8,128)(2,1)S(1)}, bf16[128,2048]{1,0:T(8,128)(2,1)S(1)}, u32[]{:S(2)}, u32[]{:S(2)}) collective-permute-start(bf16[128,2048]{1,0:T(8,128)(2,1)S(1)} %bitcast.95), channel_id=1, source_target_pairs={{15,0},{0,1},{1,2},{2,3},{3,4},{4,5},{5,6},{6,7},{7,8},{8,9},{9,10... | collective-permute-start | bytes 1572872 | tf_op jit(solution)/shard_map/ppermute | solution.py:17
  63.4 23.6 %collective-permute-start.7 = (bf16[64,2048]{1,0:T(8,128)(2,1)}, bf16[64,2048]{1,0:T(8,128)(2,1)S(1)}, u32[]{:S(2)}, u32[]{:S(2)}) collective-permute-start(bf16[64,2048]{1,0:T(8,128)(2,1)} %bitcast.5), channel_id=1, source_target_pairs={{14,0},{15,1},{0,2},{1,3},{2,4},{3,5},{4,6},{5,7},{6,8},{7,9},{8,1... | collective-permute-start | bytes 786440 | tf_op jit(solution)/shard_map/ppermute | solution.py:17
  84.9 12.0 %collective-permute-start.2 = (f32[192,1024]{1,0:T(8,128)}, f32[192,1024]{1,0:T(8,128)}, u32[]{:S(2)}, u32[]{:S(2)}) collective-permute-start(f32[192,1024]{1,0:T(8,128)} %fusion.5), channel_id=1, source_target_pairs={{0,64},{64,0},{1,65},{65,1},{2,66},{66,2},{3,67},{67,3},{4,68},{68... | collective-permute-start | bytes 2359304 | tf_op jit(solution)/shard_map/ppermute | solution.py:21
  86.9 2.2 %copy-start.1 = (bf16[2048,1024]{1,0:T(8,128)(2,1)S(1)}, bf16[2048,1024]{1,0:T(8,128)(2,1)}, u32[]{:S(2)}) copy-start(bf16[2048,1024]{1,0:T(8,128)(2,1)} %param.4) | copy-start | bytes 12582916
  90.6 16.9 %collective-permute-start.8 = (f32[320,1024]{1,0:T(8,128)S(1)}, f32[320,1024]{1,0:T(8,128)S(1)}, u32[]{:S(2)}, u32[]{:S(2)}) collective-permute-start(f32[320,1024]{1,0:T(8,128)S(1)} %fusion.32), channel_id=1, source_target_pairs={{0,64},{64,0},{1,65},{65,1},{2,66},{66,2},{3,67},{67,3},{4,68},{68... | collective-permute-start | bytes 3932168 | tf_op jit(solution)/shard_map/ppermute | solution.py:21
  93.0 14.4 %collective-permute-start.3 = (bf16[64,2048]{1,0:T(8,128)(2,1)S(1)}, bf16[64,2048]{1,0:T(8,128)(2,1)S(1)}, u32[]{:S(2)}, u32[]{:S(2)}) collective-permute-start(bf16[64,2048]{1,0:T(8,128)(2,1)S(1)} %bitcast.103), channel_id=1, source_target_pairs={{2,0},{3,1},{4,2},{5,3},{6,4},{7,5},{8,6},{9,7},{10,8},{11,9},{12,... | collective-permute-start | bytes 786440 | tf_op jit(solution)/shard_map/ppermute | solution.py:17
  109.3 9.3 %copy-start = (bf16[128,1024]{1,0:T(8,128)(2,1)S(1)}, bf16[128,1024]{1,0:T(8,128)(2,1)}, u32[]{:S(2)}) copy-start(bf16[128,1024]{1,0:T(8,128)(2,1)} %param.5) | copy-start | bytes 786436
  109.3 18.4 %collective-permute-start.9 = (f32[128,1024]{1,0:T(8,128)S(1)}, f32[128,1024]{1,0:T(8,128)S(1)}, u32[]{:S(2)}, u32[]{:S(2)}) collective-permute-start(f32[128,1024]{1,0:T(8,128)S(1)} %pad_maximum_fusion.3), channel_id=1, source_target_pairs={{0,256},{128,384},{256,0},{384,128},{1,257},{129,385},{257,1},{385... | collective-permute-start | bytes 1572872 | tf_op jit(solution)/shard_map/ppermute | solution.py:25
  111.4 26.5 %collective-permute-start.10 = (f32[128,1024]{1,0:T(8,128)S(1)}, f32[128,1024]{1,0:T(8,128)S(1)}, u32[]{:S(2)}, u32[]{:S(2)}) collective-permute-start(f32[128,1024]{1,0:T(8,128)S(1)} %pad_maximum_fusion.4), channel_id=1, source_target_pairs={{0,128},{128,256},{256,384},{384,0},{1,129},{129,257},{257,385},{3... | collective-permute-start | bytes 1572872 | tf_op jit(solution)/shard_map/ppermute | solution.py:25
  115.2 22.7 %collective-permute-start.11 = (f32[128,1024]{1,0:T(8,128)}, f32[128,1024]{1,0:T(8,128)S(1)}, u32[]{:S(2)}, u32[]{:S(2)}) collective-permute-start(f32[128,1024]{1,0:T(8,128)} %pad_maximum_fusion.5), channel_id=1, source_target_pairs={{0,384},{128,0},{256,128},{384,256},{1,385},{129,1},{257,129},{385... | collective-permute-start | bytes 1572872 | tf_op jit(solution)/shard_map/ppermute | solution.py:25

commit v2 on v1

--- a/solution.py
+++ b/solution.py
@@ -54,8 +54,9 @@
     c_plus = along_z(c_own, 1)
     c_minus = along_z(c_own, -1)
     a_all = spread(a_own, ("x", "y"), by_owner)
-    c_two_a = along_z(c_own[:64], 2)
-    c_two_b = along_z(c_own[64:], -2)
+    halves = c_own[:64], c_own[64:]
+    c_two_a = along_z(halves[0], 2)
+    c_two_b = along_z(halves[1], -2)
 
     def chips(parts):
         total = parts[0]
@@ -63,19 +64,22 @@
             total += send_x(parts[k], k)
         return total
 
-    def early(half):
-        return product(jnp.concatenate([part[half] for part in (c_own, c_plus, c_minus)]), weight)
-
-    away = from_core(early(slice(64, 128)))
-    early = (early(slice(0, 64)) + away).reshape(3, 4, 16, 1024)
+    early = [product(part, weight) for part in (c_own, c_plus, c_minus)]
+    early_away = jnp.concatenate([part[64:] for part in early])
+    early_away = from_core(early_away).reshape(3, 4, 16, 1024)
 
     def late(c_rows, a_rows):
         rows = jnp.concatenate([c_rows.reshape(4, 16, 2048), a_rows], axis=1)
         return product(rows.reshape(320, 2048), weight)
 
-    away = from_core(late(c_two_b, a_all[:, 1]))
-    late = (late(c_two_a, a_all[:, 0]) + away).reshape(4, 80, 1024)
-    sums = [jnp.concatenate([*early[:, k], late[k]]) for k in range(4)]
+    late_away = from_core(late(c_two_b, a_all[:, 1]))
+    late_away = late_away.reshape(4, 80, 1024)
+    late_kept = lax.optimization_barrier(late(c_two_a, a_all[:, 0]))
+    sums = []
+    for k in range(4):
+        own = [part[16 * k : 16 * k + 16] for part in early]
+        own = jnp.concatenate([*own, late_kept[80 * k : 80 * k + 80]])
+        sums.append(own + jnp.concatenate([*early_away[:, k], late_away[k]]))
     sums = chips(sums)
 
     c_logits = [sums[:16], sums[16:32], sums[48:64], sums[32:48]]

time: 169 us -> 161 us (0.953)
  the two profiles are of different devices: /device:TPU:4 before, /device:TPU:6 now
where the time goes in v2:
time: 161 us; the launch traced here: 160 us
  blocking collectives  60.6 us (38%)
  starting transfers between devices  51 us (32%)
  waiting for transfers between devices  24.6 us (15%)
  local copies, waits for them, and re-layouts  8.37 us (5%)
  matrix products  7.46 us (5%)
  other arithmetic  6.65 us (4%)
    all_to_all x2, blocking collectives, spread(): lax.all_to_all(jnp.broadcast_to(value[None], (size, *value.shape)), axes,...  60.6 us
    ppermute x7, starting transfers between devices, along_z(): return lax.ppermute(value, Z, [((i + by) % 16, i) for i in range(16)])  26 us
    ppermute x3, waiting for transfers between devices, send_x(): return lax.ppermute(value, 'x', [(i, (i + by) % 4) for i in range(4)])  18.8 us
    all_to_all x2, starting transfers between devices, spread(): lax.all_to_all(jnp.broadcast_to(value[None], (size, *value.shape)), axes,...  11.3 us
    ppermute x3, starting transfers between devices, send_x(): return lax.ppermute(value, 'x', [(i, (i + by) % 4) for i in range(4)])  9.42 us
    dot_general x5, matrix products, product(): return jnp.dot(rows, weight, preferred_element_type=jnp.float32)  7.46 us
    ppermute x7, waiting for transfers between devices, along_z(): return lax.ppermute(value, Z, [((i + by) % 16, i) for i in range(16)])  5.74 us
    ppermute x2, starting transfers between devices, from_core(): return lax.ppermute(value, 'core', [(0, 1), (1, 0)])  4.32 us
  transfers between devices with their start and end apart: 14, of which 6 were waited for; matrix products, arithmetic and copies ran while one was open for 8% of the time, Pallas kernels for 0%

profile of v2, /device:TPU:6, one launch (start us, length us, event | category | flops | bytes accessed | tf_op | source)
XLA Modules:
  0.0 159.8 jit_solution(6063074907510116300)
XLA Ops:
  0.6 0.9 broadcast_in_dim.10
  1.5 31.0 %all_to_all.20 = bf16[4,16,2048]{2,1,0:T(8,128)(2,1)S(1)} all-to-all(bf16[4,16,2048]{2,1,0:T(8,128)(2,1)S(1)} %broadcast_in_dim.10), channel_id=1, replica_groups={{0,4,8,12},{72,76,64,68},{1,5,9,13},{73,77,65,69},{2,6,10,14},{74,78,66..., dimensions={0} | all-to-all | bytes 524288 | tf_op jit(solution)/shard_map/all_to_all | solution.py:11
  32.5 0.8 broadcast_in_dim.11
  33.3 6.5 %all-to-all-start.1 = ((bf16[4,4,8,2048]{3,2,1,0:T(8,128)(2,1)}), bf16[4,4,8,2048]{3,2,1,0:T(8,128)(2,1)S(1)}, u32[]{:S(2)}, u32[]{:S(2)}) async-start(bf16[4,4,8,2048]{3,2,1,0:T(8,128)(2,1)} %broadcast_in_dim.11), calls=%async_computation.1 | async-start | bytes 1048576 | tf_op jit(solution)/shard_map/all_to_all | solution.py:11
  39.8 3.5 %collective-permute-start.4 = (bf16[4,8,2048]{2,1,0:T(8,128)(2,1)S(1)}, bf16[4,8,2048]{2,1,0:T(8,128)(2,1)S(1)}, u32[]{:S(2)}, u32[]{:S(2)}) collective-permute-start(bf16[4,8,2048]{2,1,0:T(8,128)(2,1)S(1)} %get-tuple-element.48), channel_id=1, source_target_pairs={{2,0},{3,1},{4,2},{5,3},{6,4},{7,5},{8,6},{9,7},{10,8},{11,9},{12,... | collective-permute-start | bytes 393224 | tf_op jit(solution)/shard_map/ppermute | solution.py:17
  43.3 2.9 %collective-permute-start.5 = (bf16[4,8,2048]{2,1,0:T(8,128)(2,1)S(1)}, bf16[4,8,2048]{2,1,0:T(8,128)(2,1)S(1)}, u32[]{:S(2)}, u32[]{:S(2)}) collective-permute-start(bf16[4,8,2048]{2,1,0:T(8,128)(2,1)S(1)} %get-tuple-element.48), channel_id=1, source_target_pairs={{15,0},{0,1},{1,2},{2,3},{3,4},{4,5},{5,6},{6,7},{7,8},{8,9},{9,10... | collective-permute-start | bytes 393224 | tf_op jit(solution)/shard_map/ppermute | solution.py:17
  46.2 4.2 %collective-permute-start.3 = (bf16[4,8,2048]{2,1,0:T(8,128)(2,1)S(1)}, bf16[4,8,2048]{2,1,0:T(8,128)(2,1)S(1)}, u32[]{:S(2)}, u32[]{:S(2)}) collective-permute-start(bf16[4,8,2048]{2,1,0:T(8,128)(2,1)S(1)} %get-tuple-element.48), channel_id=1, source_target_pairs={{1,0},{2,1},{3,2},{4,3},{5,4},{6,5},{7,6},{8,7},{9,8},{10,9},{11,1... | collective-permute-start | bytes 393224 | tf_op jit(solution)/shard_map/ppermute | solution.py:17
  50.3 0.0 collective-permute-done.4
  50.4 1.0 collective-permute-done.5
  51.3 1.7 %collective-permute-done.3 = bf16[4,8,2048]{2,1,0:T(8,128)(2,1)S(1)} collective-permute-done((bf16[4,8,2048]{2,1,0:T(8,128)(2,1)S(1)}, bf16[4,8,2048]{2,1,0:T(8,128)(2,1)S(1)}, u32[]{:S(2)}, u32[]{:S(2)}) %collective-permute-start.3) | collective-permute-done | bytes 131104 | tf_op jit(solution)/shard_map/ppermute | solution.py:17
  53.0 0.1 pad_maximum_fusion.3
  53.1 0.0 all-to-all-done.1
  53.1 1.6 %broadcast_in_dim.13 = bf16[4,2,64,2048]{3,2,1,0:T(8,128)(2,1)} broadcast(bf16[2,64,2048]{2,1,0:T(8,128)(2,1)S(1)} %bitcast.96), dimensions={1,2,3} | broadcast | bytes 2621440 | tf_op jit(solution)/shard_map/broadcast_in_dim | solution.py:12
  54.7 4.8 %all-to-all-start.2 = ((bf16[4,2,64,2048]{3,2,1,0:T(8,128)(2,1)}), bf16[4,2,64,2048]{3,2,1,0:T(8,128)(2,1)S(1)}, u32[]{:S(2)}, u32[]{:S(2)}) async-start(bf16[4,2,64,2048]{3,2,1,0:T(8,128)(2,1)} %broadcast_in_dim.13), calls=%async_computation.2 | async-start | bytes 4194304 | tf_op jit(solution)/shard_map/all_to_all | solution.py:11
  59.5 0.8 fusion.19
  60.4 5.4 %collective-permute-start = (bf16[128,2048]{1,0:T(8,128)(2,1)S(1)}, bf16[128,2048]{1,0:T(8,128)(2,1)S(1)}, u32[]{:S(2)}, u32[]{:S(2)}) collective-permute-start(bf16[128,2048]{1,0:T(8,128)(2,1)S(1)} %bitcast.93), channel_id=1, source_target_pairs={{1,0},{2,1},{3,2},{4,3},{5,4},{6,5},{7,6},{8,7},{9,8},{10,9},{11,1... | collective-permute-start | bytes 1572872 | tf_op jit(solution)/shard_map/ppermute | solution.py:17
  65.8 1.9 %collective-permute-start.1 = (bf16[128,2048]{1,0:T(8,128)(2,1)S(1)}, bf16[128,2048]{1,0:T(8,128)(2,1)S(1)}, u32[]{:S(2)}, u32[]{:S(2)}) collective-permute-start(bf16[128,2048]{1,0:T(8,128)(2,1)S(1)} %bitcast.94), channel_id=1, source_target_pairs={{15,0},{0,1},{1,2},{2,3},{3,4},{4,5},{5,6},{6,7},{7,8},{8,9},{9,10... | collective-permute-start | bytes 1572872 | tf_op jit(solution)/shard_map/ppermute | solution.py:17
  67.7 4.8 %collective-permute-start.7 = (bf16[64,2048]{1,0:T(8,128)(2,1)}, bf16[64,2048]{1,0:T(8,128)(2,1)S(1)}, u32[]{:S(2)}, u32[]{:S(2)}) collective-permute-start(bf16[64,2048]{1,0:T(8,128)(2,1)} %bitcast.20), channel_id=1, source_target_pairs={{14,0},{15,1},{0,2},{1,3},{2,4},{3,5},{4,6},{5,7},{6,8},{7,9},{8,1... | collective-permute-start | bytes 786440 | tf_op jit(solution)/shard_map/ppermute | solution.py:17
  72.5 0.0 copy-start
  72.5 3.4 %collective-permute-start.2 = (bf16[64,2048]{1,0:T(8,128)(2,1)}, bf16[64,2048]{1,0:T(8,128)(2,1)}, u32[]{:S(2)}, u32[]{:S(2)}) collective-permute-start(bf16[64,2048]{1,0:T(8,128)(2,1)} %bitcast.4), channel_id=1, source_target_pairs={{2,0},{3,1},{4,2},{5,3},{6,4},{7,5},{8,6},{9,7},{10,8},{11,9},{12,... | collective-permute-start | bytes 786440 | tf_op jit(solution)/shard_map/ppermute | solution.py:17
  75.9 2.9 %fusion.22 = f32[128,1024]{1,0:T(8,128)S(1)} fusion(bf16[128,2048]{1,0:T(8,128)(2,1)S(1)} %bitcast.95, bf16[2048,1024]{1,0:T(8,128)(2,1)} %param.4), kind=kOutput, calls=%fused_computation.66 | convolution fusion | flops 536870912 | bytes 5242880 | tf_op jit(solution)/shard_map/dot_general | solution.py:29
  78.9 0.0 copy-start.3
  78.9 0.7 fusion.16
  79.7 0.0 collective-permute-done
  79.7 0.7 fusion.23
  80.4 0.0 slice-start
  80.4 3.1 %collective-permute-done.1 = bf16[128,2048]{1,0:T(8,128)(2,1)S(1)} collective-permute-done((bf16[128,2048]{1,0:T(8,128)(2,1)S(1)}, bf16[128,2048]{1,0:T(8,128)(2,1)S(1)}, u32[]{:S(2)}, u32[]{:S(2)}) %collective-permute-start.1) | collective-permute-done | bytes 524320 | tf_op jit(solution)/shard_map/ppermute | solution.py:17
  83.5 0.7 fusion.24
  84.3 1.0 pad_maximum_fusion.2
  85.2 1.9 %collective-permute-start.6 = (f32[192,1024]{1,0:T(8,128)}, f32[192,1024]{1,0:T(8,128)}, u32[]{:S(2)}, u32[]{:S(2)}) collective-permute-start(f32[192,1024]{1,0:T(8,128)} %pad_maximum_fusion.2), channel_id=1, source_target_pairs={{0,64},{64,0},{1,65},{65,1},{2,66},{66,2},{3,67},{67,3},{4,68},{68... | collective-permute-start | bytes 2359304 | tf_op jit(solution)/shard_map/ppermute | solution.py:21
  87.1 0.0 all-to-all-done.2
  87.1 0.2 slice_bitcast_fusion
  87.4 0.0 collective-permute-done.7
  87.4 0.0 copy-start.1
  87.4 1.4 pad_maximum_fusion
  88.9 0.8 copy-done.1
  89.7 1.5 fusion.26
  91.2 2.4 %collective-permute-start.8 = (f32[320,1024]{1,0:T(8,128)S(1)}, f32[320,1024]{1,0:T(8,128)S(1)}, u32[]{:S(2)}, u32[]{:S(2)}) collective-permute-start(f32[320,1024]{1,0:T(8,128)S(1)} %fusion.26), channel_id=1, source_target_pairs={{0,64},{64,0},{1,65},{65,1},{2,66},{66,2},{3,67},{67,3},{4,68},{68... | collective-permute-start | bytes 3932168 | tf_op jit(solution)/shard_map/ppermute | solution.py:21
  93.7 1.5 fusion.25
  95.2 0.0 collective-permute-done.6
  95.3 1.2 slice_bitcast_fusion.17
  96.5 0.1 fusion.15
  96.6 0.0 collective-permute-done.8
  96.7 0.1 fusion.14
  96.8 0.5 copy-done.5
  97.3 0.1 maximum_add_fusion.1
  97.4 2.0 %collective-permute-start.9 = (f32[128,1024]{1,0:T(8,128)S(1)}, f32[128,1024]{1,0:T(8,128)S(1)}, u32[]{:S(2)}, u32[]{:S(2)}) collective-permute-start(f32[128,1024]{1,0:T(8,128)S(1)} %maximum_add_fusion.1), channel_id=1, source_target_pairs={{0,256},{128,384},{256,0},{384,128},{1,257},{129,385},{257,1},{385... | collective-permute-start | bytes 1572872 | tf_op jit(solution)/shard_map/ppermute | solution.py:25
  99.4 0.1 maximum_add_fusion.2
  99.5 5.5 %collective-permute-start.10 = (f32[128,1024]{1,0:T(8,128)S(1)}, f32[128,1024]{1,0:T(8,128)}, u32[]{:S(2)}, u32[]{:S(2)}) collective-permute-start(f32[128,1024]{1,0:T(8,128)S(1)} %maximum_add_fusion.2), channel_id=1, source_target_pairs={{0,128},{128,256},{256,384},{384,0},{1,129},{129,257},{257,385},{3... | collective-permute-start | bytes 1572872 | tf_op jit(solution)/shard_map/ppermute | solution.py:25
  105.0 0.1 maximum_add_fusion.3
  105.1 1.9 %collective-permute-start.11 = (f32[128,1024]{1,0:T(8,128)S(1)}, f32[128,1024]{1,0:T(8,128)}, u32[]{:S(2)}, u32[]{:S(2)}) collective-permute-start(f32[128,1024]{1,0:T(8,128)S(1)} %maximum_add_fusion.3), channel_id=1, source_target_pairs={{0,384},{128,0},{256,128},{384,256},{1,385},{129,1},{257,129},{385... | collective-permute-start | bytes 1572872 | tf_op jit(solution)/shard_map/ppermute | solution.py:25
  107.0 0.1 reduce_max.42
  107.1 8.5 %collective-permute-done.9 = f32[128,1024]{1,0:T(8,128)S(1)} collective-permute-done((f32[128,1024]{1,0:T(8,128)S(1)}, f32[128,1024]{1,0:T(8,128)S(1)}, u32[]{:S(2)}, u32[]{:S(2)}) %collective-permute-start.9) | collective-permute-done | bytes 524320 | tf_op jit(solution)/shard_map/ppermute | solution.py:25
  115.6 8.2 %collective-permute-done.10 = f32[128,1024]{1,0:T(8,128)} collective-permute-done((f32[128,1024]{1,0:T(8,128)S(1)}, f32[128,1024]{1,0:T(8,128)}, u32[]{:S(2)}, u32[]{:S(2)}) %collective-permute-start.10) | collective-permute-done | bytes 524320 | tf_op jit(solution)/shard_map/ppermute | solution.py:25
  123.8 2.2 %collective-permute-done.11 = f32[128,1024]{1,0:T(8,128)} collective-permute-done((f32[128,1024]{1,0:T(8,128)S(1)}, f32[128,1024]{1,0:T(8,128)}, u32[]{:S(2)}, u32[]{:S(2)}) %collective-permute-start.11) | collective-permute-done | bytes 524320 | tf_op jit(solution)/shard_map/ppermute | solution.py:25
  126.0 1.4 fusion.11
  127.5 0.2 fusion.12
  127.7 0.2 exponential_reduce_fusion
  127.9 0.1 add.84
  128.0 0.3 fusion.2
  128.4 29.6 %all_to_all.21 = f32[64,3,128]{2,1,0:T(4,128)S(1)} all-to-all(f32[64,3,128]{2,1,0:T(4,128)S(1)} %broadcast_in_dim.14), channel_id=1, replica_groups=mesh['x'=4,'core'=2,'y'=4,'zh'=4,'zl'=4] {'y','zh','zl'}, dimensions={0} | all-to-all | bytes 196608 | tf_op jit(solution)/shard_map/all_to_all | solution.py:11
  158.0 0.1 fusion.21
  158.2 1.0 fusion.5
  159.3 0.5 add_add_fusion
  (31 shorter events, 0.5 us)
Async XLA Ops:
  33.3 19.8 %all-to-all-start.1 = ((bf16[4,4,8,2048]{3,2,1,0:T(8,128)(2,1)}), bf16[4,4,8,2048]{3,2,1,0:T(8,128)(2,1)S(1)}, u32[]{:S(2)}, u32[]{:S(2)}) async-start(bf16[4,4,8,2048]{3,2,1,0:T(8,128)(2,1)} %broadcast_in_dim.11), calls=%async_computation.1 | async-start | bytes 1048576 | tf_op jit(solution)/shard_map/all_to_all | solution.py:11
  39.8 10.5 %collective-permute-start.4 = (bf16[4,8,2048]{2,1,0:T(8,128)(2,1)S(1)}, bf16[4,8,2048]{2,1,0:T(8,128)(2,1)S(1)}, u32[]{:S(2)}, u32[]{:S(2)}) collective-permute-start(bf16[4,8,2048]{2,1,0:T(8,128)(2,1)S(1)} %get-tuple-element.48), channel_id=1, source_target_pairs={{2,0},{3,1},{4,2},{5,3},{6,4},{7,5},{8,6},{9,7},{10,8},{11,9},{12,... | collective-permute-start | bytes 393224 | tf_op jit(solution)/shard_map/ppermute | solution.py:17
  43.3 8.1 %collective-permute-start.5 = (bf16[4,8,2048]{2,1,0:T(8,128)(2,1)S(1)}, bf16[4,8,2048]{2,1,0:T(8,128)(2,1)S(1)}, u32[]{:S(2)}, u32[]{:S(2)}) collective-permute-start(bf16[4,8,2048]{2,1,0:T(8,128)(2,1)S(1)} %get-tuple-element.48), channel_id=1, source_target_pairs={{15,0},{0,1},{1,2},{2,3},{3,4},{4,5},{5,6},{6,7},{7,8},{8,9},{9,10... | collective-permute-start | bytes 393224 | tf_op jit(solution)/shard_map/ppermute | solution.py:17
  46.2 6.9 %collective-permute-start.3 = (bf16[4,8,2048]{2,1,0:T(8,128)(2,1)S(1)}, bf16[4,8,2048]{2,1,0:T(8,128)(2,1)S(1)}, u32[]{:S(2)}, u32[]{:S(2)}) collective-permute-start(bf16[4,8,2048]{2,1,0:T(8,128)(2,1)S(1)} %get-tuple-element.48), channel_id=1, source_target_pairs={{1,0},{2,1},{3,2},{4,3},{5,4},{6,5},{7,6},{8,7},{9,8},{10,9},{11,1... | collective-permute-start | bytes 393224 | tf_op jit(solution)/shard_map/ppermute | solution.py:17
  54.7 32.4 %all-to-all-start.2 = ((bf16[4,2,64,2048]{3,2,1,0:T(8,128)(2,1)}), bf16[4,2,64,2048]{3,2,1,0:T(8,128)(2,1)S(1)}, u32[]{:S(2)}, u32[]{:S(2)}) async-start(bf16[4,2,64,2048]{3,2,1,0:T(8,128)(2,1)} %broadcast_in_dim.13), calls=%async_computation.2 | async-start | bytes 4194304 | tf_op jit(solution)/shard_map/all_to_all | solution.py:11
  60.4 19.3 %collective-permute-start = (bf16[128,2048]{1,0:T(8,128)(2,1)S(1)}, bf16[128,2048]{1,0:T(8,128)(2,1)S(1)}, u32[]{:S(2)}, u32[]{:S(2)}) collective-permute-start(bf16[128,2048]{1,0:T(8,128)(2,1)S(1)} %bitcast.93), channel_id=1, source_target_pairs={{1,0},{2,1},{3,2},{4,3},{5,4},{6,5},{7,6},{8,7},{9,8},{10,9},{11,1... | collective-permute-start | bytes 1572872 | tf_op jit(solution)/shard_map/ppermute | solution.py:17
  65.8 17.7 %collective-permute-start.1 = (bf16[128,2048]{1,0:T(8,128)(2,1)S(1)}, bf16[128,2048]{1,0:T(8,128)(2,1)S(1)}, u32[]{:S(2)}, u32[]{:S(2)}) collective-permute-start(bf16[128,2048]{1,0:T(8,128)(2,1)S(1)} %bitcast.94), channel_id=1, source_target_pairs={{15,0},{0,1},{1,2},{2,3},{3,4},{4,5},{5,6},{6,7},{7,8},{8,9},{9,10... | collective-permute-start | bytes 1572872 | tf_op jit(solution)/shard_map/ppermute | solution.py:17
  67.7 19.7 %collective-permute-start.7 = (bf16[64,2048]{1,0:T(8,128)(2,1)}, bf16[64,2048]{1,0:T(8,128)(2,1)S(1)}, u32[]{:S(2)}, u32[]{:S(2)}) collective-permute-start(bf16[64,2048]{1,0:T(8,128)(2,1)} %bitcast.20), channel_id=1, source_target_pairs={{14,0},{15,1},{0,2},{1,3},{2,4},{3,5},{4,6},{5,7},{6,8},{7,9},{8,1... | collective-permute-start | bytes 786440 | tf_op jit(solution)/shard_map/ppermute | solution.py:17
  72.5 7.2 %copy-start = (bf16[2048,1024]{1,0:T(8,128)(2,1)S(1)}, bf16[2048,1024]{1,0:T(8,128)(2,1)}, u32[]{:S(2)}) copy-start(bf16[2048,1024]{1,0:T(8,128)(2,1)} %param.4) | copy-start | bytes 12582916
  72.5 14.9 %collective-permute-start.2 = (bf16[64,2048]{1,0:T(8,128)(2,1)}, bf16[64,2048]{1,0:T(8,128)(2,1)}, u32[]{:S(2)}, u32[]{:S(2)}) collective-permute-start(bf16[64,2048]{1,0:T(8,128)(2,1)} %bitcast.4), channel_id=1, source_target_pairs={{2,0},{3,1},{4,2},{5,3},{6,4},{7,5},{8,6},{9,7},{10,8},{11,9},{12,... | collective-permute-start | bytes 786440 | tf_op jit(solution)/shard_map/ppermute | solution.py:17
  78.9 1.5 copy-start.3
  80.4 3.8 %slice-start = ((f32[128,1024]{1,0:T(8,128)}), f32[64,1024]{1,0:T(8,128)S(1)}, s32[]{:S(2)}) async-start(f32[128,1024]{1,0:T(8,128)} %copy-done.3), calls=%async_computation.4 | async-start | bytes 524288 | tf_op jit(solution)/shard_map/slice | solution.py:68
  85.2 10.0 %collective-permute-start.6 = (f32[192,1024]{1,0:T(8,128)}, f32[192,1024]{1,0:T(8,128)}, u32[]{:S(2)}, u32[]{:S(2)}) collective-permute-start(f32[192,1024]{1,0:T(8,128)} %pad_maximum_fusion.2), channel_id=1, source_target_pairs={{0,64},{64,0},{1,65},{65,1},{2,66},{66,2},{3,67},{67,3},{4,68},{68... | collective-permute-start | bytes 2359304 | tf_op jit(solution)/shard_map/ppermute | solution.py:21
  87.4 2.3 %copy-start.1 = (bf16[2048,1024]{1,0:T(8,128)(2,1)S(1)}, bf16[2048,1024]{1,0:T(8,128)(2,1)}, u32[]{:S(2)}) copy-start(bf16[2048,1024]{1,0:T(8,128)(2,1)} %param.4) | copy-start | bytes 12582916
  91.2 5.4 %collective-permute-start.8 = (f32[320,1024]{1,0:T(8,128)S(1)}, f32[320,1024]{1,0:T(8,128)S(1)}, u32[]{:S(2)}, u32[]{:S(2)}) collective-permute-start(f32[320,1024]{1,0:T(8,128)S(1)} %fusion.26), channel_id=1, source_target_pairs={{0,64},{64,0},{1,65},{65,1},{2,66},{66,2},{3,67},{67,3},{4,68},{68... | collective-permute-start | bytes 3932168 | tf_op jit(solution)/shard_map/ppermute | solution.py:21
  96.5 0.8 copy-start.5
  96.6 2.8 %copy-start.4 = (f32[16,1024]{1,0:T(8,128)S(1)}, f32[16,1024]{1,0:T(8,128)}, u32[]{:S(2)}) copy-start(f32[16,1024]{1,0:T(8,128)} %get-tuple-element.34) | copy-start | bytes 196612
  97.3 9.7 %copy-start.2 = (bf16[128,1024]{1,0:T(8,128)(2,1)S(1)}, bf16[128,1024]{1,0:T(8,128)(2,1)}, u32[]{:S(2)}) copy-start(bf16[128,1024]{1,0:T(8,128)(2,1)} %param.5) | copy-start | bytes 786436
  97.4 18.2 %collective-permute-start.9 = (f32[128,1024]{1,0:T(8,128)S(1)}, f32[128,1024]{1,0:T(8,128)S(1)}, u32[]{:S(2)}, u32[]{:S(2)}) collective-permute-start(f32[128,1024]{1,0:T(8,128)S(1)} %maximum_add_fusion.1), channel_id=1, source_target_pairs={{0,256},{128,384},{256,0},{384,128},{1,257},{129,385},{257,1},{385... | collective-permute-start | bytes 1572872 | tf_op jit(solution)/shard_map/ppermute | solution.py:25
  99.5 24.3 %collective-permute-start.10 = (f32[128,1024]{1,0:T(8,128)S(1)}, f32[128,1024]{1,0:T(8,128)}, u32[]{:S(2)}, u32[]{:S(2)}) collective-permute-start(f32[128,1024]{1,0:T(8,128)S(1)} %maximum_add_fusion.2), channel_id=1, source_target_pairs={{0,128},{128,256},{256,384},{384,0},{1,129},{129,257},{257,385},{3... | collective-permute-start | bytes 1572872 | tf_op jit(solution)/shard_map/ppermute | solution.py:25
  105.1 20.9 %collective-permute-start.11 = (f32[128,1024]{1,0:T(8,128)S(1)}, f32[128,1024]{1,0:T(8,128)}, u32[]{:S(2)}, u32[]{:S(2)}) collective-permute-start(f32[128,1024]{1,0:T(8,128)S(1)} %maximum_add_fusion.3), channel_id=1, source_target_pairs={{0,384},{128,0},{256,128},{384,256},{1,385},{129,1},{257,129},{385... | collective-permute-start | bytes 1572872 | tf_op jit(solution)/shard_map/ppermute | solution.py:25

commit v3 on v2

--- a/solution.py
+++ b/solution.py
@@ -15,6 +15,10 @@
 
 def along_z(value, by):
     return lax.ppermute(value, Z, [((i + by) % 16, i) for i in range(16)])
+
+
+def across_z(value):
+    return lax.ppermute(value, Z, [(i, (i + 2 - 4 * (i % 2)) % 16) for i in range(16)])
 
 
 def from_core(value):
@@ -48,15 +52,14 @@
     by_owner = [[4 * x + (x + k) % 4 for k in range(4)] for x in range(4)]
     c_own = spread(second, ("x", "y"), by_owner)
     c_own = c_own.reshape(4, 2, 16, 2048).transpose(1, 0, 2, 3).reshape(128, 2048)
-    near = [first] + [along_z(first, k) for k in (2, 1, -1)]
+    near = [first, across_z(first)]
+    near += [along_z(first, k) for k in (1, -1)]
     a_own = jnp.stack([near[n] for n in (0, 2, 1, 3)], axis=1).reshape(2, 64, 2048)
 
     c_plus = along_z(c_own, 1)
     c_minus = along_z(c_own, -1)
     a_all = spread(a_own, ("x", "y"), by_owner)
-    halves = c_own[:64], c_own[64:]
-    c_two_a = along_z(halves[0], 2)
-    c_two_b = along_z(halves[1], -2)
+    c_two = across_z(c_own)
 
     def chips(parts):
         total = parts[0]
@@ -65,21 +68,21 @@
         return total
 
     early = [product(part, weight) for part in (c_own, c_plus, c_minus)]
-    early_away = jnp.concatenate([part[64:] for part in early])
-    early_away = from_core(early_away).reshape(3, 4, 16, 1024)
+    early_away = jnp.concatenate([part[64:].reshape(4, 16, 1024) for part in early], axis=1)
+    early_away = from_core(early_away.reshape(192, 1024))
 
     def late(c_rows, a_rows):
         rows = jnp.concatenate([c_rows.reshape(4, 16, 2048), a_rows], axis=1)
         return product(rows.reshape(320, 2048), weight)
 
-    late_away = from_core(late(c_two_b, a_all[:, 1]))
-    late_away = late_away.reshape(4, 80, 1024)
-    late_kept = lax.optimization_barrier(late(c_two_a, a_all[:, 0]))
+    late_away = from_core(late(c_two[64:], a_all[:, 1]))
+    late_kept = lax.optimization_barrier(late(c_two[:64], a_all[:, 0]))
     sums = []
     for k in range(4):
         own = [part[16 * k : 16 * k + 16] for part in early]
         own = jnp.concatenate([*own, late_kept[80 * k : 80 * k + 80]])
-        sums.append(own + jnp.concatenate([*early_away[:, k], late_away[k]]))
+        away = [early_away[48 * k : 48 * k + 48], late_away[80 * k : 80 * k + 80]]
+        sums.append(own + jnp.concatenate(away))
     sums = chips(sums)
 
     c_logits = [sums[:16], sums[16:32], sums[48:64], sums[32:48]]

time: 161 us -> 164 us (1.019)
  waiting for transfers between devices: 24.6 us -> 35.6 us
  starting transfers between devices: 51 us -> 44.3 us
  local copies, waits for them, and re-layouts: 8.37 us -> 10.1 us
    ppermute x7 -> x4, starting transfers between devices: 26 us -> 12.9 us  [along_z(): return lax.ppermute(value, Z, [((i + by) % 16, i) for i in range(16)])]
    ppermute x0 -> x2, starting transfers between devices: none -> 6.41 us  [across_z(): lax.ppermute(value, Z, [(i, (i + 2 - 4 * (i % 2)) % 16) for i in range(16)])]
    ppermute x7 -> x4, waiting for transfers between devices: 5.74 us -> 12.1 us  [along_z(): return lax.ppermute(value, Z, [((i + by) % 16, i) for i in range(16)])]
    ppermute x0 -> x2, waiting for transfers between devices: none -> 4.65 us  [across_z(): lax.ppermute(value, Z, [(i, (i + 2 - 4 * (i % 2)) % 16) for i in range(16)])]
    unnamed x12 -> x14, local copies, waits for them, and re-layouts: 1.35 us -> 3.09 us
  transfers between devices with their start and end apart: 14 -> 13, of which waited for: 6 -> 7; matrix products, arithmetic and copies ran while one was open for 8% -> 8% of each run, Pallas kernels for 0% -> 0%
where the time goes in v3:
time: 164 us; the launch traced here: 163 us
  blocking collectives  59.1 us (36%)
  starting transfers between devices  44.3 us (27%)
  waiting for transfers between devices  35.6 us (22%)
  local copies, waits for them, and re-layouts  10.1 us (6%)
  matrix products  7.47 us (5%)
  other arithmetic  5.55 us (3%)
    all_to_all x2, blocking collectives, spread(): lax.all_to_all(jnp.broadcast_to(value[None], (size, *value.shape)), axes,...  59.1 us
    ppermute x3, waiting for transfers between devices, send_x(): return lax.ppermute(value, 'x', [(i, (i + by) % 4) for i in range(4)])  18.8 us
    ppermute x4, starting transfers between devices, along_z(): return lax.ppermute(value, Z, [((i + by) % 16, i) for i in range(16)])  12.9 us
    ppermute x4, waiting for transfers between devices, along_z(): return lax.ppermute(value, Z, [((i + by) % 16, i) for i in range(16)])  12.1 us
    all_to_all x2, starting transfers between devices, spread(): lax.all_to_all(jnp.broadcast_to(value[None], (size, *value.shape)), axes,...  11.3 us
    ppermute x3, starting transfers between devices, send_x(): return lax.ppermute(value, 'x', [(i, (i + by) % 4) for i in range(4)])  9.42 us
    dot_general x5, matrix products, product(): return jnp.dot(rows, weight, preferred_element_type=jnp.float32)  7.47 us
    ppermute x2, starting transfers between devices, across_z(): lax.ppermute(value, Z, [(i, (i + 2 - 4 * (i % 2)) % 16) for i in range(16)])  6.41 us
  transfers between devices with their start and end apart: 13, of which 7 were waited for; matrix products, arithmetic and copies ran while one was open for 8% of the time, Pallas kernels for 0%

profile of v3, /device:TPU:6, one launch (start us, length us, event | category | flops | bytes accessed | tf_op | source)
XLA Modules:
  0.0 163.2 jit_solution(2164606496019791549)
XLA Ops:
  0.6 0.9 broadcast_in_dim.10
  1.5 31.0 %all_to_all.20 = bf16[4,16,2048]{2,1,0:T(8,128)(2,1)S(1)} all-to-all(bf16[4,16,2048]{2,1,0:T(8,128)(2,1)S(1)} %broadcast_in_dim.10), channel_id=1, replica_groups={{0,4,8,12},{72,76,64,68},{1,5,9,13},{73,77,65,69},{2,6,10,14},{74,78,66..., dimensions={0} | all-to-all | bytes 524288 | tf_op jit(solution)/shard_map/all_to_all | solution.py:11
  32.5 0.8 broadcast_in_dim.11
  33.3 6.5 %all-to-all-start.1 = ((bf16[4,4,8,2048]{3,2,1,0:T(8,128)(2,1)}), bf16[4,4,8,2048]{3,2,1,0:T(8,128)(2,1)S(1)}, u32[]{:S(2)}, u32[]{:S(2)}) async-start(bf16[4,4,8,2048]{3,2,1,0:T(8,128)(2,1)} %broadcast_in_dim.11), calls=%async_computation.1 | async-start | bytes 1048576 | tf_op jit(solution)/shard_map/all_to_all | solution.py:11
  39.8 4.4 %collective-permute-start.5 = (bf16[4,8,2048]{2,1,0:T(8,128)(2,1)S(1)}, bf16[4,8,2048]{2,1,0:T(8,128)(2,1)S(1)}, u32[]{:S(2)}, u32[]{:S(2)}) collective-permute-start(bf16[4,8,2048]{2,1,0:T(8,128)(2,1)S(1)} %get-tuple-element.40), channel_id=1, source_target_pairs={{15,0},{0,1},{1,2},{2,3},{3,4},{4,5},{5,6},{6,7},{7,8},{8,9},{9,10... | collective-permute-start | bytes 393224 | tf_op jit(solution)/shard_map/ppermute | solution.py:17
  44.2 2.6 %collective-permute-start.3 = (bf16[4,8,2048]{2,1,0:T(8,128)(2,1)S(1)}, bf16[4,8,2048]{2,1,0:T(8,128)(2,1)S(1)}, u32[]{:S(2)}, u32[]{:S(2)}) collective-permute-start(bf16[4,8,2048]{2,1,0:T(8,128)(2,1)S(1)} %get-tuple-element.40), channel_id=1, source_target_pairs={{1,0},{2,1},{3,2},{4,3},{5,4},{6,5},{7,6},{8,7},{9,8},{10,9},{11,1... | collective-permute-start | bytes 393224 | tf_op jit(solution)/shard_map/ppermute | solution.py:17
  46.9 3.7 %collective-permute-start.4 = (bf16[4,8,2048]{2,1,0:T(8,128)(2,1)S(1)}, bf16[4,8,2048]{2,1,0:T(8,128)(2,1)S(1)}, u32[]{:S(2)}, u32[]{:S(2)}) collective-permute-start(bf16[4,8,2048]{2,1,0:T(8,128)(2,1)S(1)} %get-tuple-element.40), channel_id=1, source_target_pairs={{0,2},{1,15},{2,4},{3,1},{4,6},{5,3},{6,8},{7,5},{8,10},{9,7},{10,... | collective-permute-start | bytes 393224 | tf_op jit(solution)/shard_map/ppermute | solution.py:21
  50.5 0.0 collective-permute-done.5
  50.6 0.6 collective-permute-done.3
  51.2 4.6 %collective-permute-done.4 = bf16[4,8,2048]{2,1,0:T(8,128)(2,1)S(1)} collective-permute-done((bf16[4,8,2048]{2,1,0:T(8,128)(2,1)S(1)}, bf16[4,8,2048]{2,1,0:T(8,128)(2,1)S(1)}, u32[]{:S(2)}, u32[]{:S(2)}) %collective-permute-start.4) | collective-permute-done | bytes 131104 | tf_op jit(solution)/shard_map/ppermute | solution.py:21
  55.8 0.1 pad_maximum_fusion.3
  55.9 0.0 all-to-all-done.1
  55.9 1.6 broadcast_in_dim.13
  57.5 4.8 %all-to-all-start.2 = ((bf16[4,2,64,2048]{3,2,1,0:T(8,128)(2,1)}), bf16[4,2,64,2048]{3,2,1,0:T(8,128)(2,1)S(1)}, u32[]{:S(2)}, u32[]{:S(2)}) async-start(bf16[4,2,64,2048]{3,2,1,0:T(8,128)(2,1)} %broadcast_in_dim.13), calls=%async_computation.2 | async-start | bytes 4194304 | tf_op jit(solution)/shard_map/all_to_all | solution.py:11
  62.4 0.0 copy-start
  62.4 2.7 %collective-permute-start.2 = (bf16[128,2048]{1,0:T(8,128)(2,1)S(1)}, bf16[128,2048]{1,0:T(8,128)(2,1)S(1)}, u32[]{:S(2)}, u32[]{:S(2)}) collective-permute-start(bf16[128,2048]{1,0:T(8,128)(2,1)S(1)} %bitcast.68), channel_id=1, source_target_pairs={{0,2},{1,15},{2,4},{3,1},{4,6},{5,3},{6,8},{7,5},{8,10},{9,7},{10,... | collective-permute-start | bytes 1572872 | tf_op jit(solution)/shard_map/ppermute | solution.py:21
  65.1 1.9 %collective-permute-start = (bf16[128,2048]{1,0:T(8,128)(2,1)S(1)}, bf16[128,2048]{1,0:T(8,128)(2,1)S(1)}, u32[]{:S(2)}, u32[]{:S(2)}) collective-permute-start(bf16[128,2048]{1,0:T(8,128)(2,1)S(1)} %bitcast.69), channel_id=1, source_target_pairs={{1,0},{2,1},{3,2},{4,3},{5,4},{6,5},{7,6},{8,7},{9,8},{10,9},{11,1... | collective-permute-start | bytes 1572872 | tf_op jit(solution)/shard_map/ppermute | solution.py:17
  67.0 3.9 %collective-permute-start.1 = (bf16[128,2048]{1,0:T(8,128)(2,1)S(1)}, bf16[128,2048]{1,0:T(8,128)(2,1)S(1)}, u32[]{:S(2)}, u32[]{:S(2)}) collective-permute-start(bf16[128,2048]{1,0:T(8,128)(2,1)S(1)} %bitcast.70), channel_id=1, source_target_pairs={{15,0},{0,1},{1,2},{2,3},{3,4},{4,5},{5,6},{6,7},{7,8},{8,9},{9,10... | collective-permute-start | bytes 1572872 | tf_op jit(solution)/shard_map/ppermute | solution.py:17
  71.0 2.9 %fusion.23 = f32[128,1024]{1,0:T(8,128)S(1)} fusion(bf16[128,2048]{1,0:T(8,128)(2,1)S(1)} %bitcast.71, bf16[2048,1024]{1,0:T(8,128)(2,1)} %param.4), kind=kOutput, calls=%fused_computation.55 | convolution fusion | flops 536870912 | bytes 5242880 | tf_op jit(solution)/shard_map/dot_general | solution.py:33
  73.9 0.0 copy-start.3
  73.9 0.7 fusion.17
  74.7 10.4 %collective-permute-done = bf16[128,2048]{1,0:T(8,128)(2,1)S(1)} collective-permute-done((bf16[128,2048]{1,0:T(8,128)(2,1)S(1)}, bf16[128,2048]{1,0:T(8,128)(2,1)S(1)}, u32[]{:S(2)}, u32[]{:S(2)}) %collective-permute-start) | collective-permute-done | bytes 524320 | tf_op jit(solution)/shard_map/ppermute | solution.py:17
  85.1 0.7 fusion.24
  85.8 0.0 copy-done.3
  85.8 0.0 slice-start
  85.8 1.1 collective-permute-done.1
  87.0 0.7 fusion.25
  87.7 1.0 pad_maximum_fusion.2
  88.7 1.9 %collective-permute-start.6 = (f32[192,1024]{1,0:T(8,128)}, f32[192,1024]{1,0:T(8,128)}, u32[]{:S(2)}, u32[]{:S(2)}) collective-permute-start(f32[192,1024]{1,0:T(8,128)} %bitcast.17), channel_id=1, source_target_pairs={{0,64},{64,0},{1,65},{65,1},{2,66},{66,2},{3,67},{67,3},{4,68},{68... | collective-permute-start | bytes 2359304 | tf_op jit(solution)/shard_map/ppermute | solution.py:25
  90.6 0.0 collective-permute-done.2
  90.6 0.7 fusion.20
  91.4 0.0 all-to-all-done.2
  91.4 0.2 slice_bitcast_fusion
  91.6 0.7 copy-done.4
  92.3 0.3 pad_maximum_fusion
  92.7 1.8 %copy-done.1 = bf16[2048,1024]{1,0:T(8,128)(2,1)S(1)} copy-done((bf16[2048,1024]{1,0:T(8,128)(2,1)S(1)}, bf16[2048,1024]{1,0:T(8,128)(2,1)}, u32[]{:S(2)}) %copy-start.1) | copy-done | bytes 4194328
  94.5 1.5 fusion.27
  96.0 2.4 %collective-permute-start.7 = (f32[320,1024]{1,0:T(8,128)S(1)}, f32[320,1024]{1,0:T(8,128)S(1)}, u32[]{:S(2)}, u32[]{:S(2)}) collective-permute-start(f32[320,1024]{1,0:T(8,128)S(1)} %fusion.27), channel_id=1, source_target_pairs={{0,64},{64,0},{1,65},{65,1},{2,66},{66,2},{3,67},{67,3},{4,68},{68... | collective-permute-start | bytes 3932168 | tf_op jit(solution)/shard_map/ppermute | solution.py:25
  98.5 1.5 fusion.26
  100.1 0.0 collective-permute-done.6
  100.1 1.3 fusion.16
  101.4 0.1 fusion.15
  101.5 0.0 collective-permute-done.7
  101.5 0.1 fusion.14
  101.7 0.5 copy-done.6
  102.2 0.1 maximum_add_fusion.1
  102.3 1.9 %collective-permute-start.8 = (f32[128,1024]{1,0:T(8,128)S(1)}, f32[128,1024]{1,0:T(8,128)S(1)}, u32[]{:S(2)}, u32[]{:S(2)}) collective-permute-start(f32[128,1024]{1,0:T(8,128)S(1)} %maximum_add_fusion.1), channel_id=1, source_target_pairs={{0,256},{128,384},{256,0},{384,128},{1,257},{129,385},{257,1},{385... | collective-permute-start | bytes 1572872 | tf_op jit(solution)/shard_map/ppermute | solution.py:29
  104.2 0.1 maximum_add_fusion.2
  104.3 5.6 %collective-permute-start.9 = (f32[128,1024]{1,0:T(8,128)S(1)}, f32[128,1024]{1,0:T(8,128)}, u32[]{:S(2)}, u32[]{:S(2)}) collective-permute-start(f32[128,1024]{1,0:T(8,128)S(1)} %maximum_add_fusion.2), channel_id=1, source_target_pairs={{0,128},{128,256},{256,384},{384,0},{1,129},{129,257},{257,385},{3... | collective-permute-start | bytes 1572872 | tf_op jit(solution)/shard_map/ppermute | solution.py:29
  109.8 0.1 maximum_add_fusion.3
  109.9 1.9 %collective-permute-start.10 = (f32[128,1024]{1,0:T(8,128)S(1)}, f32[128,1024]{1,0:T(8,128)}, u32[]{:S(2)}, u32[]{:S(2)}) collective-permute-start(f32[128,1024]{1,0:T(8,128)S(1)} %maximum_add_fusion.3), channel_id=1, source_target_pairs={{0,384},{128,0},{256,128},{384,256},{1,385},{129,1},{257,129},{385... | collective-permute-start | bytes 1572872 | tf_op jit(solution)/shard_map/ppermute | solution.py:29
  111.9 0.1 reduce_max.42
  112.0 8.5 %collective-permute-done.8 = f32[128,1024]{1,0:T(8,128)S(1)} collective-permute-done((f32[128,1024]{1,0:T(8,128)S(1)}, f32[128,1024]{1,0:T(8,128)S(1)}, u32[]{:S(2)}, u32[]{:S(2)}) %collective-permute-start.8) | collective-permute-done | bytes 524320 | tf_op jit(solution)/shard_map/ppermute | solution.py:29
  120.5 8.2 %collective-permute-done.9 = f32[128,1024]{1,0:T(8,128)} collective-permute-done((f32[128,1024]{1,0:T(8,128)S(1)}, f32[128,1024]{1,0:T(8,128)}, u32[]{:S(2)}, u32[]{:S(2)}) %collective-permute-start.9) | collective-permute-done | bytes 524320 | tf_op jit(solution)/shard_map/ppermute | solution.py:29
  128.6 2.2 %collective-permute-done.10 = f32[128,1024]{1,0:T(8,128)} collective-permute-done((f32[128,1024]{1,0:T(8,128)S(1)}, f32[128,1024]{1,0:T(8,128)}, u32[]{:S(2)}, u32[]{:S(2)}) %collective-permute-start.10) | collective-permute-done | bytes 524320 | tf_op jit(solution)/shard_map/ppermute | solution.py:29
  130.8 1.4 fusion.11
  132.3 0.2 fusion.12
  132.6 0.2 exponential_reduce_fusion
  132.8 0.1 add.84
  132.9 0.3 fusion.2
  133.2 28.2 %all_to_all.21 = f32[64,3,128]{2,1,0:T(4,128)S(1)} all-to-all(f32[64,3,128]{2,1,0:T(4,128)S(1)} %broadcast_in_dim.14), channel_id=1, replica_groups=mesh['x'=4,'core'=2,'y'=4,'zh'=4,'zl'=4] {'y','zh','zl'}, dimensions={0} | all-to-all | bytes 196608 | tf_op jit(solution)/shard_map/all_to_all | solution.py:11
  161.4 0.1 fusion.22
  161.6 1.0 fusion.5
  162.7 0.5 add_add_fusion
  (31 shorter events, 0.5 us)
Async XLA Ops:
  33.3 22.6 %all-to-all-start.1 = ((bf16[4,4,8,2048]{3,2,1,0:T(8,128)(2,1)}), bf16[4,4,8,2048]{3,2,1,0:T(8,128)(2,1)S(1)}, u32[]{:S(2)}, u32[]{:S(2)}) async-start(bf16[4,4,8,2048]{3,2,1,0:T(8,128)(2,1)} %broadcast_in_dim.11), calls=%async_computation.1 | async-start | bytes 1048576 | tf_op jit(solution)/shard_map/all_to_all | solution.py:11
  39.8 10.7 %collective-permute-start.5 = (bf16[4,8,2048]{2,1,0:T(8,128)(2,1)S(1)}, bf16[4,8,2048]{2,1,0:T(8,128)(2,1)S(1)}, u32[]{:S(2)}, u32[]{:S(2)}) collective-permute-start(bf16[4,8,2048]{2,1,0:T(8,128)(2,1)S(1)} %get-tuple-element.40), channel_id=1, source_target_pairs={{15,0},{0,1},{1,2},{2,3},{3,4},{4,5},{5,6},{6,7},{7,8},{8,9},{9,10... | collective-permute-start | bytes 393224 | tf_op jit(solution)/shard_map/ppermute | solution.py:17
  44.2 6.9 %collective-permute-start.3 = (bf16[4,8,2048]{2,1,0:T(8,128)(2,1)S(1)}, bf16[4,8,2048]{2,1,0:T(8,128)(2,1)S(1)}, u32[]{:S(2)}, u32[]{:S(2)}) collective-permute-start(bf16[4,8,2048]{2,1,0:T(8,128)(2,1)S(1)} %get-tuple-element.40), channel_id=1, source_target_pairs={{1,0},{2,1},{3,2},{4,3},{5,4},{6,5},{7,6},{8,7},{9,8},{10,9},{11,1... | collective-permute-start | bytes 393224 | tf_op jit(solution)/shard_map/ppermute | solution.py:17
  46.9 9.0 %collective-permute-start.4 = (bf16[4,8,2048]{2,1,0:T(8,128)(2,1)S(1)}, bf16[4,8,2048]{2,1,0:T(8,128)(2,1)S(1)}, u32[]{:S(2)}, u32[]{:S(2)}) collective-permute-start(bf16[4,8,2048]{2,1,0:T(8,128)(2,1)S(1)} %get-tuple-element.40), channel_id=1, source_target_pairs={{0,2},{1,15},{2,4},{3,1},{4,6},{5,3},{6,8},{7,5},{8,10},{9,7},{10,... | collective-permute-start | bytes 393224 | tf_op jit(solution)/shard_map/ppermute | solution.py:21
  57.5 33.8 %all-to-all-start.2 = ((bf16[4,2,64,2048]{3,2,1,0:T(8,128)(2,1)}), bf16[4,2,64,2048]{3,2,1,0:T(8,128)(2,1)S(1)}, u32[]{:S(2)}, u32[]{:S(2)}) async-start(bf16[4,2,64,2048]{3,2,1,0:T(8,128)(2,1)} %broadcast_in_dim.13), calls=%async_computation.2 | async-start | bytes 4194304 | tf_op jit(solution)/shard_map/all_to_all | solution.py:11
  62.4 22.7 %copy-start = (bf16[2048,1024]{1,0:T(8,128)(2,1)S(1)}, bf16[2048,1024]{1,0:T(8,128)(2,1)}, u32[]{:S(2)}) copy-start(bf16[2048,1024]{1,0:T(8,128)(2,1)} %param.4) | copy-start | bytes 12582916
  62.4 28.2 %collective-permute-start.2 = (bf16[128,2048]{1,0:T(8,128)(2,1)S(1)}, bf16[128,2048]{1,0:T(8,128)(2,1)S(1)}, u32[]{:S(2)}, u32[]{:S(2)}) collective-permute-start(bf16[128,2048]{1,0:T(8,128)(2,1)S(1)} %bitcast.68), channel_id=1, source_target_pairs={{0,2},{1,15},{2,4},{3,1},{4,6},{5,3},{6,8},{7,5},{8,10},{9,7},{10,... | collective-permute-start | bytes 1572872 | tf_op jit(solution)/shard_map/ppermute | solution.py:21
  65.1 19.9 %collective-permute-start = (bf16[128,2048]{1,0:T(8,128)(2,1)S(1)}, bf16[128,2048]{1,0:T(8,128)(2,1)S(1)}, u32[]{:S(2)}, u32[]{:S(2)}) collective-permute-start(bf16[128,2048]{1,0:T(8,128)(2,1)S(1)} %bitcast.69), channel_id=1, source_target_pairs={{1,0},{2,1},{3,2},{4,3},{5,4},{6,5},{7,6},{8,7},{9,8},{10,9},{11,1... | collective-permute-start | bytes 1572872 | tf_op jit(solution)/shard_map/ppermute | solution.py:17
  67.0 19.9 %collective-permute-start.1 = (bf16[128,2048]{1,0:T(8,128)(2,1)S(1)}, bf16[128,2048]{1,0:T(8,128)(2,1)S(1)}, u32[]{:S(2)}, u32[]{:S(2)}) collective-permute-start(bf16[128,2048]{1,0:T(8,128)(2,1)S(1)} %bitcast.70), channel_id=1, source_target_pairs={{15,0},{0,1},{1,2},{2,3},{3,4},{4,5},{5,6},{6,7},{7,8},{8,9},{9,10... | collective-permute-start | bytes 1572872 | tf_op jit(solution)/shard_map/ppermute | solution.py:17
  73.9 11.9 %copy-start.3 = (f32[128,1024]{1,0:T(8,128)}, f32[128,1024]{1,0:T(8,128)S(1)}, u32[]{:S(2)}) copy-start(f32[128,1024]{1,0:T(8,128)S(1)} %fusion.23) | copy-start | bytes 1572868
  85.8 1.9 %slice-start = ((f32[128,1024]{1,0:T(8,128)}), f32[64,1024]{1,0:T(8,128)S(1)}, s32[]{:S(2)}) async-start(f32[128,1024]{1,0:T(8,128)} %copy-done.3), calls=%async_computation.4 | async-start | bytes 524288 | tf_op jit(solution)/shard_map/slice | solution.py:71
  88.7 11.4 %collective-permute-start.6 = (f32[192,1024]{1,0:T(8,128)}, f32[192,1024]{1,0:T(8,128)}, u32[]{:S(2)}, u32[]{:S(2)}) collective-permute-start(f32[192,1024]{1,0:T(8,128)} %bitcast.17), channel_id=1, source_target_pairs={{0,64},{64,0},{1,65},{65,1},{2,66},{66,2},{3,67},{67,3},{4,68},{68... | collective-permute-start | bytes 2359304 | tf_op jit(solution)/shard_map/ppermute | solution.py:25
  91.4 1.0 copy-start.4
  92.3 2.2 %copy-start.1 = (bf16[2048,1024]{1,0:T(8,128)(2,1)S(1)}, bf16[2048,1024]{1,0:T(8,128)(2,1)}, u32[]{:S(2)}) copy-start(bf16[2048,1024]{1,0:T(8,128)(2,1)} %param.4) | copy-start | bytes 12582916
  96.0 5.5 %collective-permute-start.7 = (f32[320,1024]{1,0:T(8,128)S(1)}, f32[320,1024]{1,0:T(8,128)S(1)}, u32[]{:S(2)}, u32[]{:S(2)}) collective-permute-start(f32[320,1024]{1,0:T(8,128)S(1)} %fusion.27), channel_id=1, source_target_pairs={{0,64},{64,0},{1,65},{65,1},{2,66},{66,2},{3,67},{67,3},{4,68},{68... | collective-permute-start | bytes 3932168 | tf_op jit(solution)/shard_map/ppermute | solution.py:25
  101.3 0.8 copy-start.6
  101.5 2.7 %copy-start.5 = (f32[16,1024]{1,0:T(8,128)S(1)}, f32[16,1024]{1,0:T(8,128)}, u32[]{:S(2)}) copy-start(f32[16,1024]{1,0:T(8,128)} %get-tuple-element.26) | copy-start | bytes 196612
  102.2 9.7 %copy-start.2 = (bf16[128,1024]{1,0:T(8,128)(2,1)S(1)}, bf16[128,1024]{1,0:T(8,128)(2,1)}, u32[]{:S(2)}) copy-start(bf16[128,1024]{1,0:T(8,128)(2,1)} %param.5) | copy-start | bytes 786436
  102.3 18.2 %collective-permute-start.8 = (f32[128,1024]{1,0:T(8,128)S(1)}, f32[128,1024]{1,0:T(8,128)S(1)}, u32[]{:S(2)}, u32[]{:S(2)}) collective-permute-start(f32[128,1024]{1,0:T(8,128)S(1)} %maximum_add_fusion.1), channel_id=1, source_target_pairs={{0,256},{128,384},{256,0},{384,128},{1,257},{129,385},{257,1},{385... | collective-permute-start | bytes 1572872 | tf_op jit(solution)/shard_map/ppermute | solution.py:29
  104.3 24.4 %collective-permute-start.9 = (f32[128,1024]{1,0:T(8,128)S(1)}, f32[128,1024]{1,0:T(8,128)}, u32[]{:S(2)}, u32[]{:S(2)}) collective-permute-start(f32[128,1024]{1,0:T(8,128)S(1)} %maximum_add_fusion.2), channel_id=1, source_target_pairs={{0,128},{128,256},{256,384},{384,0},{1,129},{129,257},{257,385},{3... | collective-permute-start | bytes 1572872 | tf_op jit(solution)/shard_map/ppermute | solution.py:29
  109.9 20.9 %collective-permute-start.10 = (f32[128,1024]{1,0:T(8,128)S(1)}, f32[128,1024]{1,0:T(8,128)}, u32[]{:S(2)}, u32[]{:S(2)}) collective-permute-start(f32[128,1024]{1,0:T(8,128)S(1)} %maximum_add_fusion.3), channel_id=1, source_target_pairs={{0,384},{128,0},{256,128},{384,256},{1,385},{129,1},{257,129},{385... | collective-permute-start | bytes 1572872 | tf_op jit(solution)/shard_map/ppermute | solution.py:29

commit v4 on v3

--- a/solution.py
+++ b/solution.py
@@ -67,21 +67,22 @@
             total += send_x(parts[k], k)
         return total
 
-    early = [product(part, weight) for part in (c_own, c_plus, c_minus)]
+    early = [product(part, weight) for part in (c_own, c_plus)]
     early_away = jnp.concatenate([part[64:].reshape(4, 16, 1024) for part in early], axis=1)
-    early_away = from_core(early_away.reshape(192, 1024))
+    early_away = from_core(early_away.reshape(128, 1024))
 
-    def late(c_rows, a_rows):
-        rows = jnp.concatenate([c_rows.reshape(4, 16, 2048), a_rows], axis=1)
-        return product(rows.reshape(320, 2048), weight)
+    def late(side):
+        rows = [part.reshape(2, 4, 16, 2048)[side] for part in (c_minus, c_two)]
+        rows = jnp.concatenate([*rows, a_all[:, side]], axis=1)
+        return product(rows.reshape(384, 2048), weight)
 
-    late_away = from_core(late(c_two[64:], a_all[:, 1]))
-    late_kept = lax.optimization_barrier(late(c_two[:64], a_all[:, 0]))
+    late_away = from_core(late(1))
+    late_kept = lax.optimization_barrier(late(0))
     sums = []
     for k in range(4):
         own = [part[16 * k : 16 * k + 16] for part in early]
-        own = jnp.concatenate([*own, late_kept[80 * k : 80 * k + 80]])
-        away = [early_away[48 * k : 48 * k + 48], late_away[80 * k : 80 * k + 80]]
+        own = jnp.concatenate([*own, late_kept[96 * k : 96 * k + 96]])
+        away = [early_away[32 * k : 32 * k + 32], late_away[96 * k : 96 * k + 96]]
         sums.append(own + jnp.concatenate(away))
     sums = chips(sums)
 

time: 164 us -> 160 us (0.976)
  waiting for transfers between devices: 35.6 us -> 29.9 us
    ppermute x4, waiting for transfers between devices: 12.1 us -> 5.2 us  [along_z(): return lax.ppermute(value, Z, [((i + by) % 16, i) for i in range(16)])]
    ppermute x2, starting transfers between devices: 6.41 us -> 8.79 us  [across_z(): lax.ppermute(value, Z, [(i, (i + 2 - 4 * (i % 2)) % 16) for i in range(16)])]
    dot_general x5 -> x4, matrix products: 7.47 us -> 8.41 us  [product(): return jnp.dot(rows, weight, preferred_element_type=jnp.float32)]
  transfers between devices with their start and end apart: 13 -> 13, of which waited for: 7 -> 7; matrix products, arithmetic and copies ran while one was open for 8% -> 10% of each run, Pallas kernels for 0% -> 0%
where the time goes in v4:
time: 160 us; the launch traced here: 159 us
  blocking collectives  58.7 us (37%)
  starting transfers between devices  45.4 us (28%)
  waiting for transfers between devices  29.9 us (19%)
  local copies, waits for them, and re-layouts  10.4 us (6%)
  matrix products  8.41 us (5%)
  other arithmetic  5.48 us (3%)
    all_to_all x2, blocking collectives, spread(): lax.all_to_all(jnp.broadcast_to(value[None], (size, *value.shape)), axes,...  58.7 us
    ppermute x3, waiting for transfers between devices, send_x(): return lax.ppermute(value, 'x', [(i, (i + by) % 4) for i in range(4)])  19.1 us
    ppermute x4, starting transfers between devices, along_z(): return lax.ppermute(value, Z, [((i + by) % 16, i) for i in range(16)])  12.1 us
    all_to_all x2, starting transfers between devices, spread(): lax.all_to_all(jnp.broadcast_to(value[None], (size, *value.shape)), axes,...  11.3 us
    ppermute x3, starting transfers between devices, send_x(): return lax.ppermute(value, 'x', [(i, (i + by) % 4) for i in range(4)])  9.42 us
    ppermute x2, starting transfers between devices, across_z(): lax.ppermute(value, Z, [(i, (i + 2 - 4 * (i % 2)) % 16) for i in range(16)])  8.79 us
    dot_general x4, matrix products, product(): return jnp.dot(rows, weight, preferred_element_type=jnp.float32)  8.41 us
    ppermute x2, waiting for transfers between devices, across_z(): lax.ppermute(value, Z, [(i, (i + 2 - 4 * (i % 2)) % 16) for i in range(16)])  5.32 us
  transfers between devices with their start and end apart: 13, of which 7 were waited for; matrix products, arithmetic and copies ran while one was open for 10% of the time, Pallas kernels for 0%

profile of v4, /device:TPU:6, one launch (start us, length us, event | category | flops | bytes accessed | tf_op | source)
XLA Modules:
  0.0 159.3 jit_solution(7560032611302396553)
XLA Ops:
  0.6 0.9 broadcast_in_dim.10
  1.5 31.0 %all_to_all.20 = bf16[4,16,2048]{2,1,0:T(8,128)(2,1)S(1)} all-to-all(bf16[4,16,2048]{2,1,0:T(8,128)(2,1)S(1)} %broadcast_in_dim.10), channel_id=1, replica_groups={{0,4,8,12},{72,76,64,68},{1,5,9,13},{73,77,65,69},{2,6,10,14},{74,78,66..., dimensions={0} | all-to-all | bytes 524288 | tf_op jit(solution)/shard_map/all_to_all | solution.py:11
  32.5 0.8 broadcast_in_dim.11
  33.3 6.5 %all-to-all-start.1 = ((bf16[4,4,8,2048]{3,2,1,0:T(8,128)(2,1)}), bf16[4,4,8,2048]{3,2,1,0:T(8,128)(2,1)S(1)}, u32[]{:S(2)}, u32[]{:S(2)}) async-start(bf16[4,4,8,2048]{3,2,1,0:T(8,128)(2,1)} %broadcast_in_dim.11), calls=%async_computation.1 | async-start | bytes 1048576 | tf_op jit(solution)/shard_map/all_to_all | solution.py:11
  39.8 4.9 %collective-permute-start.4 = (bf16[4,8,2048]{2,1,0:T(8,128)(2,1)S(1)}, bf16[4,8,2048]{2,1,0:T(8,128)(2,1)S(1)}, u32[]{:S(2)}, u32[]{:S(2)}) collective-permute-start(bf16[4,8,2048]{2,1,0:T(8,128)(2,1)S(1)} %get-tuple-element.38), channel_id=1, source_target_pairs={{0,2},{1,15},{2,4},{3,1},{4,6},{5,3},{6,8},{7,5},{8,10},{9,7},{10,... | collective-permute-start | bytes 393224 | tf_op jit(solution)/shard_map/ppermute | solution.py:21
  44.7 1.9 %collective-permute-start.5 = (bf16[4,8,2048]{2,1,0:T(8,128)(2,1)S(1)}, bf16[4,8,2048]{2,1,0:T(8,128)(2,1)S(1)}, u32[]{:S(2)}, u32[]{:S(2)}) collective-permute-start(bf16[4,8,2048]{2,1,0:T(8,128)(2,1)S(1)} %get-tuple-element.38), channel_id=1, source_target_pairs={{15,0},{0,1},{1,2},{2,3},{3,4},{4,5},{5,6},{6,7},{7,8},{8,9},{9,10... | collective-permute-start | bytes 393224 | tf_op jit(solution)/shard_map/ppermute | solution.py:17
  46.6 5.1 %collective-permute-start.3 = (bf16[4,8,2048]{2,1,0:T(8,128)(2,1)S(1)}, bf16[4,8,2048]{2,1,0:T(8,128)(2,1)S(1)}, u32[]{:S(2)}, u32[]{:S(2)}) collective-permute-start(bf16[4,8,2048]{2,1,0:T(8,128)(2,1)S(1)} %get-tuple-element.38), channel_id=1, source_target_pairs={{1,0},{2,1},{3,2},{4,3},{5,4},{6,5},{7,6},{8,7},{9,8},{10,9},{11,1... | collective-permute-start | bytes 393224 | tf_op jit(solution)/shard_map/ppermute | solution.py:17
  51.8 0.0 all-to-all-done.1
  51.8 0.8 copy.39
  52.6 1.9 %collective-permute-start = (bf16[128,2048]{1,0:T(8,128)(2,1)}, bf16[128,2048]{1,0:T(8,128)(2,1)}, u32[]{:S(2)}, u32[]{:S(2)}) collective-permute-start(bf16[128,2048]{1,0:T(8,128)(2,1)} %bitcast.2), channel_id=1, source_target_pairs={{1,0},{2,1},{3,2},{4,3},{5,4},{6,5},{7,6},{8,7},{9,8},{10,9},{11,1... | collective-permute-start | bytes 1572872 | tf_op jit(solution)/shard_map/ppermute | solution.py:17
  54.5 0.0 collective-permute-done.4
  54.5 0.0 collective-permute-done.5
  54.5 1.1 collective-permute-done.3
  55.6 0.1 pad_maximum_fusion.2
  55.7 1.6 %broadcast_in_dim.13 = bf16[4,2,64,2048]{3,2,1,0:T(8,128)(2,1)} broadcast(bf16[2,64,2048]{2,1,0:T(8,128)(2,1)S(1)} %bitcast.67), dimensions={1,2,3} | broadcast | bytes 2621440 | tf_op jit(solution)/shard_map/broadcast_in_dim | solution.py:12
  57.3 4.8 %all-to-all-start.2 = ((bf16[4,2,64,2048]{3,2,1,0:T(8,128)(2,1)}), bf16[4,2,64,2048]{3,2,1,0:T(8,128)(2,1)S(1)}, u32[]{:S(2)}, u32[]{:S(2)}) async-start(bf16[4,2,64,2048]{3,2,1,0:T(8,128)(2,1)} %broadcast_in_dim.13), calls=%async_computation.2 | async-start | bytes 4194304 | tf_op jit(solution)/shard_map/all_to_all | solution.py:11
  62.1 3.1 %collective-permute-start.1 = (bf16[128,2048]{1,0:T(8,128)(2,1)}, bf16[128,2048]{1,0:T(8,128)(2,1)S(1)}, u32[]{:S(2)}, u32[]{:S(2)}) collective-permute-start(bf16[128,2048]{1,0:T(8,128)(2,1)} %bitcast.2), channel_id=1, source_target_pairs={{15,0},{0,1},{1,2},{2,3},{3,4},{4,5},{5,6},{6,7},{7,8},{8,9},{9,10... | collective-permute-start | bytes 1572872 | tf_op jit(solution)/shard_map/ppermute | solution.py:17
  65.2 3.9 %collective-permute-start.2 = (bf16[128,2048]{1,0:T(8,128)(2,1)}, bf16[128,2048]{1,0:T(8,128)(2,1)S(1)}, u32[]{:S(2)}, u32[]{:S(2)}) collective-permute-start(bf16[128,2048]{1,0:T(8,128)(2,1)} %bitcast.2), channel_id=1, source_target_pairs={{0,2},{1,15},{2,4},{3,1},{4,6},{5,3},{6,8},{7,5},{8,10},{9,7},{10,... | collective-permute-start | bytes 1572872 | tf_op jit(solution)/shard_map/ppermute | solution.py:21
  69.1 3.1 %fusion.23 = f32[128,1024]{1,0:T(8,128)S(1)} fusion(bf16[128,2048]{1,0:T(8,128)(2,1)} %bitcast.2, bf16[2048,1024]{1,0:T(8,128)(2,1)} %param.4), kind=kOutput, calls=%fused_computation.55 | convolution fusion | flops 536870912 | bytes 5242880 | tf_op jit(solution)/shard_map/dot_general | solution.py:33
  72.2 0.0 collective-permute-done
  72.2 0.0 copy-done
  72.3 1.8 %fusion.24 = f32[128,1024]{1,0:T(8,128)S(1)} fusion(bf16[128,2048]{1,0:T(8,128)(2,1)} %collective-permute-done, bf16[2048,1024]{1,0:T(8,128)(2,1)S(1)} %copy-done), kind=kOutput, calls=%fused_computation.56 | convolution fusion | flops 536870912 | bytes 5242880 | tf_op jit(solution)/shard_map/dot_general | solution.py:33
  74.1 0.8 pad_maximum_fusion.3
  74.9 1.9 %collective-permute-start.6 = (f32[128,1024]{1,0:T(8,128)}, f32[128,1024]{1,0:T(8,128)}, u32[]{:S(2)}, u32[]{:S(2)}) collective-permute-start(f32[128,1024]{1,0:T(8,128)} %bitcast.17), channel_id=1, source_target_pairs={{0,64},{64,0},{1,65},{65,1},{2,66},{66,2},{3,67},{67,3},{4,68},{68... | collective-permute-start | bytes 1572872 | tf_op jit(solution)/shard_map/ppermute | solution.py:25
  76.8 4.1 %collective-permute-done.1 = bf16[128,2048]{1,0:T(8,128)(2,1)S(1)} collective-permute-done((bf16[128,2048]{1,0:T(8,128)(2,1)}, bf16[128,2048]{1,0:T(8,128)(2,1)S(1)}, u32[]{:S(2)}, u32[]{:S(2)}) %collective-permute-start.1) | collective-permute-done | bytes 524320 | tf_op jit(solution)/shard_map/ppermute | solution.py:17
  80.9 0.7 fusion.19
  81.7 5.3 %collective-permute-done.2 = bf16[128,2048]{1,0:T(8,128)(2,1)S(1)} collective-permute-done((bf16[128,2048]{1,0:T(8,128)(2,1)}, bf16[128,2048]{1,0:T(8,128)(2,1)S(1)}, u32[]{:S(2)}, u32[]{:S(2)}) %collective-permute-start.2) | collective-permute-done | bytes 524320 | tf_op jit(solution)/shard_map/ppermute | solution.py:21
  87.0 0.8 fusion.20
  87.8 0.0 all-to-all-done.2
  87.8 0.1 slice_bitcast_fusion
  88.0 0.8 copy-done.3
  88.8 0.1 copy-done.4
  88.9 0.1 copy-done.5
  88.9 0.4 pad_maximum_fusion
  89.3 1.8 %copy-done.1 = bf16[2048,1024]{1,0:T(8,128)(2,1)S(1)} copy-done((bf16[2048,1024]{1,0:T(8,128)(2,1)S(1)}, bf16[2048,1024]{1,0:T(8,128)(2,1)}, u32[]{:S(2)}) %copy-start.1) | copy-done | bytes 4194328
  91.1 1.8 %fusion.26 = f32[384,1024]{1,0:T(8,128)S(1)} fusion(bf16[384,2048]{1,0:T(8,128)(2,1)S(1)} %bitcast.70, bf16[2048,1024]{1,0:T(8,128)(2,1)S(1)} %copy-done.1), kind=kOutput, calls=%fused_computation.58 | convolution fusion | flops 1610612736 | bytes 7340032 | tf_op jit(solution)/shard_map/dot_general | solution.py:33
  92.9 1.9 %collective-permute-start.7 = (f32[384,1024]{1,0:T(8,128)S(1)}, f32[384,1024]{1,0:T(8,128)S(1)}, u32[]{:S(2)}, u32[]{:S(2)}) collective-permute-start(f32[384,1024]{1,0:T(8,128)S(1)} %fusion.26), channel_id=1, source_target_pairs={{0,64},{64,0},{1,65},{65,1},{2,66},{66,2},{3,67},{67,3},{4,68},{68... | collective-permute-start | bytes 4718600 | tf_op jit(solution)/shard_map/ppermute | solution.py:25
  94.9 0.0 collective-permute-done.6
  94.9 1.1 fusion.16
  96.1 1.8 %fusion.25 = f32[384,1024]{1,0:T(8,128)S(1)} fusion(bf16[384,2048]{1,0:T(8,128)(2,1)S(1)} %bitcast.69, bf16[2048,1024]{1,0:T(8,128)(2,1)S(1)} %copy-done.1), kind=kOutput, calls=%fused_computation.57 | convolution fusion | flops 1610612736 | bytes 7340032 | tf_op jit(solution)/shard_map/dot_general | solution.py:33
  97.8 0.2 fusion.15
  98.0 0.2 collective-permute-done.7
  98.2 0.2 fusion.14
  98.4 0.0 copy-start.2
  98.4 0.1 maximum_add_fusion.1
  98.5 1.9 %collective-permute-start.8 = (f32[128,1024]{1,0:T(8,128)S(1)}, f32[128,1024]{1,0:T(8,128)S(1)}, u32[]{:S(2)}, u32[]{:S(2)}) collective-permute-start(f32[128,1024]{1,0:T(8,128)S(1)} %maximum_add_fusion.1), channel_id=1, source_target_pairs={{0,256},{128,384},{256,0},{384,128},{1,257},{129,385},{257,1},{385... | collective-permute-start | bytes 1572872 | tf_op jit(solution)/shard_map/ppermute | solution.py:29
  100.4 0.1 maximum_add_fusion.2
  100.5 5.6 %collective-permute-start.9 = (f32[128,1024]{1,0:T(8,128)S(1)}, f32[128,1024]{1,0:T(8,128)}, u32[]{:S(2)}, u32[]{:S(2)}) collective-permute-start(f32[128,1024]{1,0:T(8,128)S(1)} %maximum_add_fusion.2), channel_id=1, source_target_pairs={{0,128},{128,256},{256,384},{384,0},{1,129},{129,257},{257,385},{3... | collective-permute-start | bytes 1572872 | tf_op jit(solution)/shard_map/ppermute | solution.py:29
  106.1 0.1 maximum_add_fusion.3
  106.1 1.9 %collective-permute-start.10 = (f32[128,1024]{1,0:T(8,128)S(1)}, f32[128,1024]{1,0:T(8,128)}, u32[]{:S(2)}, u32[]{:S(2)}) collective-permute-start(f32[128,1024]{1,0:T(8,128)S(1)} %maximum_add_fusion.3), channel_id=1, source_target_pairs={{0,384},{128,0},{256,128},{384,256},{1,385},{129,1},{257,129},{385... | collective-permute-start | bytes 1572872 | tf_op jit(solution)/shard_map/ppermute | solution.py:29
  108.1 0.0 copy-done.2
  108.1 0.1 reduce_max.42
  108.2 8.5 %collective-permute-done.8 = f32[128,1024]{1,0:T(8,128)S(1)} collective-permute-done((f32[128,1024]{1,0:T(8,128)S(1)}, f32[128,1024]{1,0:T(8,128)S(1)}, u32[]{:S(2)}, u32[]{:S(2)}) %collective-permute-start.8) | collective-permute-done | bytes 524320 | tf_op jit(solution)/shard_map/ppermute | solution.py:29
  116.7 8.5 %collective-permute-done.9 = f32[128,1024]{1,0:T(8,128)} collective-permute-done((f32[128,1024]{1,0:T(8,128)S(1)}, f32[128,1024]{1,0:T(8,128)}, u32[]{:S(2)}, u32[]{:S(2)}) %collective-permute-start.9) | collective-permute-done | bytes 524320 | tf_op jit(solution)/shard_map/ppermute | solution.py:29
  125.2 2.2 %collective-permute-done.10 = f32[128,1024]{1,0:T(8,128)} collective-permute-done((f32[128,1024]{1,0:T(8,128)S(1)}, f32[128,1024]{1,0:T(8,128)}, u32[]{:S(2)}, u32[]{:S(2)}) %collective-permute-start.10) | collective-permute-done | bytes 524320 | tf_op jit(solution)/shard_map/ppermute | solution.py:29
  127.3 1.4 fusion.11
  128.8 0.2 fusion.12
  129.1 0.2 exponential_reduce_fusion
  129.3 0.1 add.84
  129.4 0.3 fusion.2
  129.8 27.8 %all_to_all.21 = f32[64,3,128]{2,1,0:T(4,128)S(1)} all-to-all(f32[64,3,128]{2,1,0:T(4,128)S(1)} %broadcast_in_dim.14), channel_id=1, replica_groups=mesh['x'=4,'core'=2,'y'=4,'zh'=4,'zl'=4] {'y','zh','zl'}, dimensions={0} | all-to-all | bytes 196608 | tf_op jit(solution)/shard_map/all_to_all | solution.py:11
  157.5 0.1 fusion.22
  157.7 1.0 fusion.5
  158.8 0.5 add_add_fusion
  (26 shorter events, 0.4 us)
Async XLA Ops:
  33.3 18.4 %all-to-all-start.1 = ((bf16[4,4,8,2048]{3,2,1,0:T(8,128)(2,1)}), bf16[4,4,8,2048]{3,2,1,0:T(8,128)(2,1)S(1)}, u32[]{:S(2)}, u32[]{:S(2)}) async-start(bf16[4,4,8,2048]{3,2,1,0:T(8,128)(2,1)} %broadcast_in_dim.11), calls=%async_computation.1 | async-start | bytes 1048576 | tf_op jit(solution)/shard_map/all_to_all | solution.py:11
  39.8 14.7 %collective-permute-start.4 = (bf16[4,8,2048]{2,1,0:T(8,128)(2,1)S(1)}, bf16[4,8,2048]{2,1,0:T(8,128)(2,1)S(1)}, u32[]{:S(2)}, u32[]{:S(2)}) collective-permute-start(bf16[4,8,2048]{2,1,0:T(8,128)(2,1)S(1)} %get-tuple-element.38), channel_id=1, source_target_pairs={{0,2},{1,15},{2,4},{3,1},{4,6},{5,3},{6,8},{7,5},{8,10},{9,7},{10,... | collective-permute-start | bytes 393224 | tf_op jit(solution)/shard_map/ppermute | solution.py:21
  44.7 9.8 %collective-permute-start.5 = (bf16[4,8,2048]{2,1,0:T(8,128)(2,1)S(1)}, bf16[4,8,2048]{2,1,0:T(8,128)(2,1)S(1)}, u32[]{:S(2)}, u32[]{:S(2)}) collective-permute-start(bf16[4,8,2048]{2,1,0:T(8,128)(2,1)S(1)} %get-tuple-element.38), channel_id=1, source_target_pairs={{15,0},{0,1},{1,2},{2,3},{3,4},{4,5},{5,6},{6,7},{7,8},{8,9},{9,10... | collective-permute-start | bytes 393224 | tf_op jit(solution)/shard_map/ppermute | solution.py:17
  46.6 9.0 %collective-permute-start.3 = (bf16[4,8,2048]{2,1,0:T(8,128)(2,1)S(1)}, bf16[4,8,2048]{2,1,0:T(8,128)(2,1)S(1)}, u32[]{:S(2)}, u32[]{:S(2)}) collective-permute-start(bf16[4,8,2048]{2,1,0:T(8,128)(2,1)S(1)} %get-tuple-element.38), channel_id=1, source_target_pairs={{1,0},{2,1},{3,2},{4,3},{5,4},{6,5},{7,6},{8,7},{9,8},{10,9},{11,1... | collective-permute-start | bytes 393224 | tf_op jit(solution)/shard_map/ppermute | solution.py:17
  52.6 19.6 %collective-permute-start = (bf16[128,2048]{1,0:T(8,128)(2,1)}, bf16[128,2048]{1,0:T(8,128)(2,1)}, u32[]{:S(2)}, u32[]{:S(2)}) collective-permute-start(bf16[128,2048]{1,0:T(8,128)(2,1)} %bitcast.2), channel_id=1, source_target_pairs={{1,0},{2,1},{3,2},{4,3},{5,4},{6,5},{7,6},{8,7},{9,8},{10,9},{11,1... | collective-permute-start | bytes 1572872 | tf_op jit(solution)/shard_map/ppermute | solution.py:17
  57.3 30.5 %all-to-all-start.2 = ((bf16[4,2,64,2048]{3,2,1,0:T(8,128)(2,1)}), bf16[4,2,64,2048]{3,2,1,0:T(8,128)(2,1)S(1)}, u32[]{:S(2)}, u32[]{:S(2)}) async-start(bf16[4,2,64,2048]{3,2,1,0:T(8,128)(2,1)} %broadcast_in_dim.13), calls=%async_computation.2 | async-start | bytes 4194304 | tf_op jit(solution)/shard_map/all_to_all | solution.py:11
  62.1 10.1 %copy-start = (bf16[2048,1024]{1,0:T(8,128)(2,1)S(1)}, bf16[2048,1024]{1,0:T(8,128)(2,1)}, u32[]{:S(2)}) copy-start(bf16[2048,1024]{1,0:T(8,128)(2,1)} %param.4) | copy-start | bytes 12582916
  62.1 18.8 %collective-permute-start.1 = (bf16[128,2048]{1,0:T(8,128)(2,1)}, bf16[128,2048]{1,0:T(8,128)(2,1)S(1)}, u32[]{:S(2)}, u32[]{:S(2)}) collective-permute-start(bf16[128,2048]{1,0:T(8,128)(2,1)} %bitcast.2), channel_id=1, source_target_pairs={{15,0},{0,1},{1,2},{2,3},{3,4},{4,5},{5,6},{6,7},{7,8},{8,9},{9,10... | collective-permute-start | bytes 1572872 | tf_op jit(solution)/shard_map/ppermute | solution.py:17
  65.2 21.8 %collective-permute-start.2 = (bf16[128,2048]{1,0:T(8,128)(2,1)}, bf16[128,2048]{1,0:T(8,128)(2,1)S(1)}, u32[]{:S(2)}, u32[]{:S(2)}) collective-permute-start(bf16[128,2048]{1,0:T(8,128)(2,1)} %bitcast.2), channel_id=1, source_target_pairs={{0,2},{1,15},{2,4},{3,1},{4,6},{5,3},{6,8},{7,5},{8,10},{9,7},{10,... | collective-permute-start | bytes 1572872 | tf_op jit(solution)/shard_map/ppermute | solution.py:21
  74.9 20.0 %collective-permute-start.6 = (f32[128,1024]{1,0:T(8,128)}, f32[128,1024]{1,0:T(8,128)}, u32[]{:S(2)}, u32[]{:S(2)}) collective-permute-start(f32[128,1024]{1,0:T(8,128)} %bitcast.17), channel_id=1, source_target_pairs={{0,64},{64,0},{1,65},{65,1},{2,66},{66,2},{3,67},{67,3},{4,68},{68... | collective-permute-start | bytes 1572872 | tf_op jit(solution)/shard_map/ppermute | solution.py:25
  87.8 1.0 copy-start.3
  87.8 1.0 copy-start.4
  87.8 1.1 copy-start.5
  88.9 2.2 %copy-start.1 = (bf16[2048,1024]{1,0:T(8,128)(2,1)S(1)}, bf16[2048,1024]{1,0:T(8,128)(2,1)}, u32[]{:S(2)}) copy-start(bf16[2048,1024]{1,0:T(8,128)(2,1)} %param.4) | copy-start | bytes 12582916
  92.9 5.3 %collective-permute-start.7 = (f32[384,1024]{1,0:T(8,128)S(1)}, f32[384,1024]{1,0:T(8,128)S(1)}, u32[]{:S(2)}, u32[]{:S(2)}) collective-permute-start(f32[384,1024]{1,0:T(8,128)S(1)} %fusion.26), channel_id=1, source_target_pairs={{0,64},{64,0},{1,65},{65,1},{2,66},{66,2},{3,67},{67,3},{4,68},{68... | collective-permute-start | bytes 4718600 | tf_op jit(solution)/shard_map/ppermute | solution.py:25
  98.4 9.7 %copy-start.2 = (bf16[128,1024]{1,0:T(8,128)(2,1)S(1)}, bf16[128,1024]{1,0:T(8,128)(2,1)}, u32[]{:S(2)}) copy-start(bf16[128,1024]{1,0:T(8,128)(2,1)} %param.5) | copy-start | bytes 786436
  98.5 18.2 %collective-permute-start.8 = (f32[128,1024]{1,0:T(8,128)S(1)}, f32[128,1024]{1,0:T(8,128)S(1)}, u32[]{:S(2)}, u32[]{:S(2)}) collective-permute-start(f32[128,1024]{1,0:T(8,128)S(1)} %maximum_add_fusion.1), channel_id=1, source_target_pairs={{0,256},{128,384},{256,0},{384,128},{1,257},{129,385},{257,1},{385... | collective-permute-start | bytes 1572872 | tf_op jit(solution)/shard_map/ppermute | solution.py:29
  100.5 24.7 %collective-permute-start.9 = (f32[128,1024]{1,0:T(8,128)S(1)}, f32[128,1024]{1,0:T(8,128)}, u32[]{:S(2)}, u32[]{:S(2)}) collective-permute-start(f32[128,1024]{1,0:T(8,128)S(1)} %maximum_add_fusion.2), channel_id=1, source_target_pairs={{0,128},{128,256},{256,384},{384,0},{1,129},{129,257},{257,385},{3... | collective-permute-start | bytes 1572872 | tf_op jit(solution)/shard_map/ppermute | solution.py:29
  106.1 21.2 %collective-permute-start.10 = (f32[128,1024]{1,0:T(8,128)S(1)}, f32[128,1024]{1,0:T(8,128)}, u32[]{:S(2)}, u32[]{:S(2)}) collective-permute-start(f32[128,1024]{1,0:T(8,128)S(1)} %maximum_add_fusion.3), channel_id=1, source_target_pairs={{0,384},{128,0},{256,128},{384,256},{1,385},{129,1},{257,129},{385... | collective-permute-start | bytes 1572872 | tf_op jit(solution)/shard_map/ppermute | solution.py:29
